TPU v7x, 512 devices: a whole 4x8x8 slice. The times are simulated.
512 devices in a mesh: tm: 256 (over z, y, x), space: 2 (over core).
Axes of the slice: x: 4, y: 8, z: 8, core: 2. Of those that a mesh axis runs over, the one named last changes fastest.
Arguments:
- image_gradient: bfloat16 [512, 128, 3, 4096], P('tm', 'space'), may hold values from -0.375 to 0.375
- residual: bfloat16 [512, 128, 4096], P('tm', 'space'), may hold values from -6 to 6
- phase: float32 [512], P('tm'), may hold values from 0 to 1
- counts: int32 [128], P('space'), may hold values from 512 to 4096
- owner: int32 [128, 1], P('space'), may hold values from 0 to 1, as said below
Outputs:
- hessian_blocks: float32 [512, 192, 576], P('tm', 'space')
- gradient_blocks: float32 [512, 192, 24], P('tm', 'space')
Inputs may be any that keep to these rules, and one draw needn't show every extreme that they name: Among the 64 bricks of each aligned block at most 48 share an owner, and one owner takes exactly 48 bricks of every block.
All inputs are finite; a program needn't handle non-finite values.
Results may differ from a plain program's by a relative error of at most 0.0029.
Values sent between devices are 32-bit elements; how exact they have to be, the bound alone decides.
A program may use at most 64 MiB of HBM per device.

v0:
```python
import jax
import jax.numpy as jnp
from jax import lax
from jax.sharding import PartitionSpec as P

EDGE = 16


def shifted(block, axis, distance):
    devices = range(lax.axis_size(axis))
    route = [(i - distance, i) for i in devices if i - distance in devices]
    return lax.ppermute(block, axis, route)


def spline_weights(phase):
    return jnp.stack(
        [
            (1.0 - phase) ** 3 / 6.0,
            (3.0 * phase**3 - 6.0 * phase**2 + 4.0) / 6.0,
            (-3.0 * phase**3 + 3.0 * phase**2 + 3.0 * phase + 1.0) / 6.0,
            phase**3 / 6.0,
        ],
        axis=-1,
    )


def shape_table(edge):
    voxel = jnp.arange(edge * edge * edge, dtype=jnp.int32)
    first = ((voxel // (edge * edge)).astype(jnp.float32) + 0.5) / edge
    second = ((voxel // edge % edge).astype(jnp.float32) + 0.5) / edge
    third = ((voxel % edge).astype(jnp.float32) + 0.5) / edge
    rows = []
    for node in range(8):
        along_first = first if node >> 2 & 1 else 1.0 - first
        along_second = second if node >> 1 & 1 else 1.0 - second
        along_third = third if node & 1 else 1.0 - third
        rows.append(along_first * along_second * along_third)
    return jnp.stack(rows, axis=0)


def per_device(image_gradient, residual, phase, counts, owner):
    step_count, brick_count, comp_count, voxel_count = image_gradient.shape
    dof_count = 8 * comp_count
    patch_width = dof_count * dof_count
    column_count = patch_width + dof_count
    first_step = lax.axis_index("tm") * step_count
    overall_step_count = lax.axis_size("tm") * step_count
    space_count = lax.axis_size("space")
    capacity = 3 * brick_count // (2 * space_count)
    valid_mask = lax.broadcasted_iota(jnp.int32, (brick_count, voxel_count), 1) < counts[:, None]
    shapes = shape_table(EDGE)

    def per_step(pair):
        grads, resid = pair
        product = shapes[None, :, None, :] * grads.astype(jnp.float32)[:, None, :, :]
        sens = product.reshape(brick_count, dof_count, voxel_count).astype(jnp.bfloat16)
        masked = jnp.where(valid_mask[:, None, :], sens, jnp.zeros((), jnp.bfloat16))
        hessian = jnp.einsum("bdv,bev->bde", masked, masked, preferred_element_type=jnp.float32)
        gradient = jnp.einsum("bdv,bv->bd", masked, resid, preferred_element_type=jnp.float32)
        return jnp.concatenate([hessian.reshape(brick_count, patch_width), gradient], axis=1)

    patch_contents = lax.map(per_step, (image_gradient, residual))
    weights = spline_weights(phase)
    global_step = first_step + jnp.arange(step_count, dtype=jnp.int32)
    target = jnp.clip(
        global_step[:, None] - 1 + jnp.arange(4, dtype=jnp.int32)[None, :],
        0,
        overall_step_count - 1,
    )
    local_slot = target - first_step + 1
    hits_table = (
        local_slot[:, :, None] == jnp.arange(step_count + 3, dtype=jnp.int32)[None, None, :]
    ).astype(jnp.float32)
    basis_lookup_grid = jnp.sum(weights[:, :, None] * hits_table, axis=1)
    is_hessian_column = (jnp.arange(column_count, dtype=jnp.int32) < patch_width)[None, None, :]
    multiplier = jnp.where(
        is_hessian_column,
        (basis_lookup_grid * basis_lookup_grid)[:, :, None],
        basis_lookup_grid[:, :, None],
    )
    owner_flat = owner[:, 0]
    owner_hits = (owner_flat[:, None] == jnp.arange(space_count, dtype=jnp.int32)[None, :]).astype(
        jnp.int32
    )
    earlier = jnp.cumsum(owner_hits, axis=0) - owner_hits
    brick_rank = jnp.sum(earlier * owner_hits, axis=1)
    destination = owner_flat * capacity + brick_rank
    slot_match = (
        destination[:, None] == jnp.arange(space_count * capacity, dtype=jnp.int32)[None, :]
    )
    source_brick = jnp.sum(
        jnp.where(slot_match, jnp.arange(brick_count, dtype=jnp.int32)[:, None], 0), axis=0
    )
    slot_filled = jnp.any(slot_match, axis=0)
    packed = multiplier[0][:, None, :] * patch_contents[0][None]
    packed = packed + multiplier[1][:, None, :] * patch_contents[1][None]
    from_before = shifted(packed[step_count + 1 :], "tm", 1)
    behind = shifted(packed[:1], "tm", -1)
    own_part = packed[1 : step_count + 1]
    own_part = own_part.at[:2].add(from_before)
    picked = jnp.take(own_part.at[step_count - 1 :].add(behind), source_brick, axis=1)
    placed = jnp.where(slot_filled[None, :, None], picked, jnp.zeros((), jnp.float32))
    result = lax.all_to_all(placed, "space", split_axis=1, concat_axis=1, tiled=True)
    return (result[:, :, :patch_width], result[:, :, patch_width:])


def solution(mesh):
    in_specs = (
        P("tm", "space", None, None),
        P("tm", "space", None),
        P("tm"),
        P("space"),
        P("space", None),
    )
    out_specs = (P("tm", "space", None), P("tm", "space", None))
    return jax.shard_map(
        per_device, mesh=mesh, in_specs=in_specs, out_specs=out_specs, check_vma=False
    )
```

profile of v0, /device:TPU:255, one launch (start us, length us, event | category | flops | bytes accessed | tf_op | source)
XLA Modules:
  0.0 134.0 jit_solution(4634049659191790835)
XLA Ops:
  1.3 102.2 %while.14 = (s32[]{:T(128)}, f32[2,64,600]{1,2,0:T(8,128)}, f32[8,4096]{1,0:T(8,128)S(1)}, bf16[2,64,3,4096]{3,1,2,0:T(8,128)(2,1)}, bf16[2,64,4096]{2,1,0:T(8,128)(2,1)}, /*index=5*/s32[64]{0:T(128)}, s32[]{:T(128)}) while((s32[]{:T(128)}, f32[2,64,600]{1,2,0:T(8,128)}, f32[8,4096]{1,0:T(8,128)S(1)}, ...), condition=%wide.region_6.7_spmd.clone, body=%wide.region_5.6_spmd.clone.sunk | while | flops 334534144 | bytes 58191368 | solution.py:62
  1.3 1.8 %bitcast_convert_fusion.2 = f32[64,3,4096]{2,0,1:T(8,128)S(1)} fusion(bf16[2,64,3,4096]{3,1,2,0:T(8,128)(2,1)} %get-tuple-element.176, s32[]{:T(128)S(6)} %copy.47), kind=kLoop, calls=%fused_computation.9.clone.1 | loop fusion | flops 786432 | bytes 4718596 | tf_op jit(solution)/shard_map/while/body/eval_jaxpr/convert_element_type | solution.py:55
  3.1 0.9 mul.344
  4.0 1.2 mul.345
  5.5 6.0 %fusion.46 = bf16[64,24,4096]{2,0,1:T(8,128)(2,1)} fusion(f32[64,3,4096]{2,0,1:T(8,128)S(1)} %bitcast_convert_fusion.2, f32[24,4096]{1,0:T(8,128)S(1)} %mul.345, pred[64,4096]{1,0:T(8,128)(4,1)S(1)} %iota_compare_fusion.6), kind=kLoop, calls=%fused_computation.4.clone.1 | loop fusion | flops 18874368 | bytes 16384000 | tf_op jit(solution)/shard_map/while/body/eval_jaxpr/jit(_where)/select_n | solution.py:57
  11.6 13.3 %fusion.47 = f32[64,1,24]{2,1,0:T(1,128)S(1)} fusion(bf16[64,24,4096]{2,0,1:T(8,128)(2,1)} %fusion.46, bf16[64,4096,1]{1,0,2:T(8,128)(2,1)S(1)} %dynamic-slice_bitcast_fusion.2), kind=kOutput, calls=%fused_computation.5.clone.1 | convolution fusion | flops 12582912 | bytes 13113344 | tf_op jit(solution)/shard_map/while/body/eval_jaxpr/bdv,bv->bd/dot_general | solution.py:59
  25.0 26.2 %fusion.48 = f32[64,24,24]{2,1,0:T(8,128)S(1)} fusion(bf16[64,24,4096]{2,0,1:T(8,128)(2,1)} %fusion.46), kind=kOutput, calls=%fused_computation.7.clone.1 | convolution fusion | flops 301989888 | bytes 12730368 | tf_op jit(solution)/shard_map/while/body/eval_jaxpr/bdv,bev->bde/dot_general | solution.py:58
  51.6 0.8 copy-done.4
  52.4 1.8 %bitcast_convert_fusion.2 = f32[64,3,4096]{2,0,1:T(8,128)S(1)} fusion(bf16[2,64,3,4096]{3,1,2,0:T(8,128)(2,1)} %get-tuple-element.176, s32[]{:T(128)S(6)} %copy.47), kind=kLoop, calls=%fused_computation.9.clone.1 | loop fusion | flops 786432 | bytes 4718596 | tf_op jit(solution)/shard_map/while/body/eval_jaxpr/convert_element_type | solution.py:55
  54.2 0.9 mul.344
  55.1 1.2 mul.345
  56.6 6.0 %fusion.46 = bf16[64,24,4096]{2,0,1:T(8,128)(2,1)} fusion(f32[64,3,4096]{2,0,1:T(8,128)S(1)} %bitcast_convert_fusion.2, f32[24,4096]{1,0:T(8,128)S(1)} %mul.345, pred[64,4096]{1,0:T(8,128)(4,1)S(1)} %iota_compare_fusion.6), kind=kLoop, calls=%fused_computation.4.clone.1 | loop fusion | flops 18874368 | bytes 16384000 | tf_op jit(solution)/shard_map/while/body/eval_jaxpr/jit(_where)/select_n | solution.py:57
  62.7 13.3 %fusion.47 = f32[64,1,24]{2,1,0:T(1,128)S(1)} fusion(bf16[64,24,4096]{2,0,1:T(8,128)(2,1)} %fusion.46, bf16[64,4096,1]{1,0,2:T(8,128)(2,1)S(1)} %dynamic-slice_bitcast_fusion.2), kind=kOutput, calls=%fused_computation.5.clone.1 | convolution fusion | flops 12582912 | bytes 13113344 | tf_op jit(solution)/shard_map/while/body/eval_jaxpr/bdv,bv->bd/dot_general | solution.py:59
  76.1 26.2 %fusion.48 = f32[64,24,24]{2,1,0:T(8,128)S(1)} fusion(bf16[64,24,4096]{2,0,1:T(8,128)(2,1)} %fusion.46), kind=kOutput, calls=%fused_computation.7.clone.1 | convolution fusion | flops 301989888 | bytes 12730368 | tf_op jit(solution)/shard_map/while/body/eval_jaxpr/bdv,bev->bde/dot_general | solution.py:58
  102.7 0.8 copy-done.4
  103.5 1.1 slice_bitcast_fusion.1
  105.6 4.3 %collective-permute-start = (f32[2,64,600]{2,0,1:T(2,128)S(1)}, f32[2,64,600]{2,0,1:T(2,128)S(1)}, u32[]{:S(2)}, u32[]{:S(2)}) collective-permute-start(f32[2,64,600]{2,0,1:T(2,128)S(1)} %slice.85), channel_id=1, source_target_pairs={{0,2},{2,4},{4,6},{6,8},{8,10},{10,12},{12,14},{14,16},{16,18},{18... | collective-permute-start | bytes 921608 | tf_op jit(solution)/shard_map/ppermute | solution.py:12
  110.1 1.9 %collective-permute-start.1 = (f32[1,64,600]{2,0,1:T(1,128)S(1)}, f32[1,64,600]{2,0,1:T(1,128)S(1)}, u32[]{:S(2)}, u32[]{:S(2)}) collective-permute-start(f32[1,64,600]{2,0,1:T(1,128)S(1)} %slice.87), channel_id=1, source_target_pairs={{2,0},{4,2},{6,4},{8,6},{10,8},{12,10},{14,12},{16,14},{18,16},{20... | collective-permute-start | bytes 460808 | tf_op jit(solution)/shard_map/ppermute | solution.py:12
  112.6 3.7 %collective-permute-done = f32[2,64,600]{2,0,1:T(2,128)S(1)} collective-permute-done((f32[2,64,600]{2,0,1:T(2,128)S(1)}, f32[2,64,600]{2,0,1:T(2,128)S(1)}, u32[]{:S(2)}, u32[]{:S(2)}) %collective-permute-start) | collective-permute-done | bytes 307232 | tf_op jit(solution)/shard_map/ppermute | solution.py:12
  116.6 5.6 %collective-permute-done.1 = f32[1,64,600]{2,0,1:T(1,128)S(1)} collective-permute-done((f32[1,64,600]{2,0,1:T(1,128)S(1)}, f32[1,64,600]{2,0,1:T(1,128)S(1)}, u32[]{:S(2)}, u32[]{:S(2)}) %collective-permute-start.1) | collective-permute-done | bytes 153632 | tf_op jit(solution)/shard_map/ppermute | solution.py:12
  122.5 2.7 %scatter-add.4 = f32[2,64,600]{2,0,1:T(2,128)S(1)} dynamic-update-slice(f32[2,64,600]{2,0,1:T(2,128)S(1)} %slice_add_fusion, f32[1,64,600]{2,0,1:T(1,128)S(1)} %slice_add_fusion.1, s32[]{:T(128)} %constant.202.clone.1, s32[]{:T(128)} %constant.192.clone.1, s32[]{:T(128)} %constant.192.clone.1) | dynamic-update-slice | bytes 307204 | tf_op jit(solution)/shard_map/scatter-add | solution.py:101
  125.2 1.1 gather_fusion
  126.7 5.5 %all_to_all.5 = f32[2,96,600]{2,0,1:T(2,128)S(1)} all-to-all(f32[2,96,600]{2,0,1:T(2,128)S(1)} %select_bitcast_fusion), channel_id=1, replica_groups=mesh['tm'=256,'space'=2] {'space'}, dimensions={1} | all-to-all | bytes 921600 | tf_op jit(solution)/shard_map/all_to_all | solution.py:103
  132.3 0.8 copy.24
  (71 shorter events, 5.2 us)
Async XLA Ops:
  1.3 103.5 %copy-start.7 = (f32[2]{0:T(128)S(1)}, f32[2]{0:T(128)}, u32[]{:S(2)}) copy-start(f32[2]{0:T(128)} %param.15) | copy-start | bytes 28
  1.3 110.8 %copy-start.6 = (s32[64,1]{0,1:T(1,128)S(1)}, s32[64,1]{0,1:T(1,128)}, u32[]{:S(2)}) copy-start(s32[64,1]{0,1:T(1,128)} %param.17) | copy-start | bytes 772
  1.3 1.8 %copy-start.1 = (f32[8,4096]{1,0:T(8,128)}, f32[8,4096]{1,0:T(8,128)S(1)}, u32[]{:S(2)}) copy-start(f32[8,4096]{1,0:T(8,128)S(1)} %get-tuple-element.175) | copy-start | bytes 393220 | tf_op jit(solution)/shard_map/while
  1.3 4.0 %copy-start.5 = (s32[64]{0:T(128)S(1)}, s32[64]{0:T(128)}, u32[]{:S(2)}) copy-start(s32[64]{0:T(128)} %get-tuple-element.178) | copy-start | bytes 772 | tf_op jit(solution)/shard_map/while
  5.5 6.1 %copy-start = (bf16[2,64,4096]{2,1,0:T(8,128)(2,1)S(1)}, bf16[2,64,4096]{2,1,0:T(8,128)(2,1)}, u32[]{:S(2)}) copy-start(bf16[2,64,4096]{2,1,0:T(8,128)(2,1)} %get-tuple-element.177) | copy-start | bytes 3145732 | tf_op jit(solution)/shard_map/while
  25.0 26.5 %copy-start.3 = (f32[2,64,600]{1,2,0:T(8,128)S(1)}, f32[2,64,600]{1,2,0:T(8,128)}, u32[]{:S(2)}) copy-start(f32[2,64,600]{1,2,0:T(8,128)} %get-tuple-element.167) | copy-start | bytes 921604 | tf_op jit(solution)/shard_map/while
  25.0 27.4 %copy-start.2 = (f32[8,4096]{1,0:T(8,128)S(1)}, f32[8,4096]{1,0:T(8,128)}, u32[]{:S(2)}) copy-start(f32[8,4096]{1,0:T(8,128)} %copy-done.1) | copy-start | bytes 393220 | tf_op jit(solution)/shard_map/while
  51.6 0.9 copy-start.4
  52.4 1.8 %copy-start.1 = (f32[8,4096]{1,0:T(8,128)}, f32[8,4096]{1,0:T(8,128)S(1)}, u32[]{:S(2)}) copy-start(f32[8,4096]{1,0:T(8,128)S(1)} %get-tuple-element.175) | copy-start | bytes 393220 | tf_op jit(solution)/shard_map/while
  52.4 4.0 %copy-start.5 = (s32[64]{0:T(128)S(1)}, s32[64]{0:T(128)}, u32[]{:S(2)}) copy-start(s32[64]{0:T(128)} %get-tuple-element.178) | copy-start | bytes 772 | tf_op jit(solution)/shard_map/while
  56.6 6.1 %copy-start = (bf16[2,64,4096]{2,1,0:T(8,128)(2,1)S(1)}, bf16[2,64,4096]{2,1,0:T(8,128)(2,1)}, u32[]{:S(2)}) copy-start(bf16[2,64,4096]{2,1,0:T(8,128)(2,1)} %get-tuple-element.177) | copy-start | bytes 3145732 | tf_op jit(solution)/shard_map/while
  76.1 26.5 %copy-start.3 = (f32[2,64,600]{1,2,0:T(8,128)S(1)}, f32[2,64,600]{1,2,0:T(8,128)}, u32[]{:S(2)}) copy-start(f32[2,64,600]{1,2,0:T(8,128)} %get-tuple-element.167) | copy-start | bytes 921604 | tf_op jit(solution)/shard_map/while
  76.1 27.4 %copy-start.2 = (f32[8,4096]{1,0:T(8,128)S(1)}, f32[8,4096]{1,0:T(8,128)}, u32[]{:S(2)}) copy-start(f32[8,4096]{1,0:T(8,128)} %copy-done.1) | copy-start | bytes 393220 | tf_op jit(solution)/shard_map/while
  102.7 0.9 copy-start.4
  105.6 10.7 %collective-permute-start = (f32[2,64,600]{2,0,1:T(2,128)S(1)}, f32[2,64,600]{2,0,1:T(2,128)S(1)}, u32[]{:S(2)}, u32[]{:S(2)}) collective-permute-start(f32[2,64,600]{2,0,1:T(2,128)S(1)} %slice.85), channel_id=1, source_target_pairs={{0,2},{2,4},{4,6},{6,8},{8,10},{10,12},{12,14},{14,16},{16,18},{18... | collective-permute-start | bytes 921608 | tf_op jit(solution)/shard_map/ppermute | solution.py:12
  110.1 12.1 %collective-permute-start.1 = (f32[1,64,600]{2,0,1:T(1,128)S(1)}, f32[1,64,600]{2,0,1:T(1,128)S(1)}, u32[]{:S(2)}, u32[]{:S(2)}) collective-permute-start(f32[1,64,600]{2,0,1:T(1,128)S(1)} %slice.87), channel_id=1, source_target_pairs={{2,0},{4,2},{6,4},{8,6},{10,8},{12,10},{14,12},{16,14},{18,16},{20... | collective-permute-start | bytes 460808 | tf_op jit(solution)/shard_map/ppermute | solution.py:12
where the time goes:
time: 134 us
  matrix products  79.1 us (59%)
  other arithmetic  18.4 us (14%)
  local copies, waits for them, and re-layouts  14.3 us (11%)
  waiting for transfers between devices  9.33 us (7%)
  starting transfers between devices  6.25 us (5%)
  blocking collectives  5.55 us (4%)
    dot_general x2, matrix products, per_step(): jnp.einsum('bdv,bev->bde', masked, masked, preferred_element_type=jnp.flo...  52.5 us
    dot_general x2, matrix products, per_step(): jnp.einsum('bdv,bv->bd', masked, resid, preferred_element_type=jnp.float32)  26.7 us
    select_n x2, other arithmetic, per_step(): jnp.where(valid_mask[:, None, :], sens, jnp.zeros((), jnp.bfloat16))  12.1 us
    ppermute x2, waiting for transfers between devices, shifted(): return lax.ppermute(block, axis, route)  9.33 us
    ppermute x2, starting transfers between devices, shifted(): return lax.ppermute(block, axis, route)  6.25 us
    all_to_all x1, blocking collectives, per_device(): lax.all_to_all(placed, 'space', split_axis=1, concat_axis=1, tiled=True)  5.55 us
    mul x4, local copies, waits for them, and re-layouts, per_step(): shapes[None, :, None, :] * grads.astype(jnp.float32)[:, None, :, :]  4.25 us
    convert_element_type x2, other arithmetic, per_step(): grads.astype(jnp.float32)[:, None, :, :]  3.61 us
  transfers between devices with their start and end apart: 2, of which 2 were waited for; matrix products, arithmetic and copies ran while one was open for 1% of the time, Pallas kernels for 0%

commit v1 on v0

v1 whole, which is shorter than its diff:
```python
import functools

import jax
import jax.numpy as jnp
import numpy as np
from jax import lax
from jax.experimental import pallas as pl
from jax.experimental.pallas import tpu as pltpu
from jax.sharding import PartitionSpec as P

EDGE = 16
COMPS = 3
NODES = 8
DOFS = NODES * COMPS
PATCH = DOFS * DOFS
MOMENTS = 27
PAIRS = ((0, 0), (0, 1), (0, 2), (1, 1), (1, 2), (2, 2))
ROWS = 80
LANES = 256
GRAD_LANE = 32 * len(PAIRS)
CHUNK = 1024
MESH = pl.DeviceIdType.MESH
F32 = jnp.float32
BF16 = jnp.bfloat16


def two_terms(table):
    high = table.astype(BF16)
    return high, (table - high.astype(np.float64)).astype(BF16)


def moment_table():
    voxel = np.arange(EDGE**3)
    axes = [voxel // (EDGE * EDGE), voxel // EDGE % EDGE, voxel % EDGE]
    u = [(axis + 0.5) / EDGE for axis in axes]
    quads = [((1 - x) ** 2, x * (1 - x), x * x) for x in u]
    lines = [(1 - x, x) for x in u]
    moments = np.stack([quads[0][m // 9] * quads[1][m // 3 % 3] * quads[2][m % 3] for m in range(MOMENTS)])
    shapes = np.stack([lines[0][a >> 2 & 1] * lines[1][a >> 1 & 1] * lines[2][a & 1] for a in range(NODES)])
    table = np.zeros((ROWS, EDGE**3), BF16)
    table[0:MOMENTS], table[32 : 32 + MOMENTS] = two_terms(moments)
    table[64:72], table[72:80] = two_terms(shapes)
    return table


def spread_tables():
    hessian = np.zeros((LANES, PATCH), np.float32)
    gradient = np.zeros((DOFS, LANES), np.float32)
    for a in range(NODES):
        for c in range(COMPS):
            gradient[COMPS * a + c, GRAD_LANE + NODES * c + a] = 1.0
            for b in range(NODES):
                for e in range(COMPS):
                    pair = PAIRS.index((min(c, e), max(c, e)))
                    bits = [(a >> s & 1) + (b >> s & 1) for s in (2, 1, 0)]
                    moment = bits[0] * 9 + bits[1] * 3 + bits[2]
                    hessian[32 * pair + moment, (COMPS * a + c) * DOFS + COMPS * b + e] = 1.0
    return hessian.astype(BF16), gradient.astype(BF16)


def split3(x):
    first = x.astype(BF16)
    rest = x - first.astype(F32)
    second = rest.astype(BF16)
    return first, second, (rest - second.astype(F32)).astype(BF16)


def dot_nt(a, b):
    return lax.dot_general(a, b, (((1,), (1,)), ((), ())), preferred_element_type=F32)


def kernel(
    n,
    image_hbm,
    resid_hbm,
    phase_hbm,
    counts_hbm,
    owner_hbm,
    table_hbm,
    spread_hbm,
    pick_hbm,
    hess_ref,
    grad_ref,
    image,
    resid,
    phase,
    counts,
    owner,
    table,
    spread,
    pick,
    mask,
    acc,
    send_fwd,
    send_back,
    send_side,
    recv_fwd,
    recv_back,
    mine,
    load_sem,
    small_sem,
    fwd_send_sem,
    fwd_recv_sem,
    back_send_sem,
    back_recv_sem,
    side_sem,
):
    bricks, voxels = resid.shape[1], resid.shape[2]
    cap = mine.shape[2]
    chunks = voxels // CHUNK
    d = lax.axis_index("tm")
    s = lax.axis_index("space")
    has_before = d > 0
    has_after = d < n - 1

    small = [
        pltpu.make_async_copy(counts_hbm, counts, small_sem.at[0]),
        pltpu.make_async_copy(owner_hbm, owner, small_sem.at[1]),
        pltpu.make_async_copy(phase_hbm, phase, small_sem.at[2]),
        pltpu.make_async_copy(spread_hbm, spread, small_sem.at[3]),
        pltpu.make_async_copy(pick_hbm, pick, small_sem.at[4]),
    ]
    small[0].start()
    loads = {}
    for t in (1, 0):
        for k in range(chunks):
            span = pl.ds(k * CHUNK, CHUNK)
            loads[t, k] = [
                pltpu.make_async_copy(
                    image_hbm.at[t, :, :, span], image.at[t, :, :, span], load_sem.at[0, t, k]
                ),
                pltpu.make_async_copy(
                    resid_hbm.at[t, :, span], resid.at[t, :, span], load_sem.at[1, t, k]
                ),
            ]
            if t == 1:
                loads[t, k].append(
                    pltpu.make_async_copy(
                        table_hbm.at[:, span], table.at[:, span], load_sem.at[2, t, k]
                    )
                )
            for copy in loads[t, k]:
                copy.start()
    for copy in small[1:]:
        copy.start()

    barrier = pltpu.get_barrier_semaphore()

    def greet(where):
        pl.semaphore_signal(barrier, inc=1, device_id=where, device_id_type=MESH)

    greet((d, 1 - s))

    @pl.when(has_before)
    def _():
        greet((d - 1, 0))
        greet((d - 1, 1))

    @pl.when(has_after)
    def _():
        greet((d + 1, 0))
        greet((d + 1, 1))

    small[0].wait()
    square = lax.broadcasted_iota(jnp.int32, (bricks, bricks), 0) == lax.broadcasted_iota(
        jnp.int32, (bricks, bricks), 1
    )
    count_column = jnp.sum(
        jnp.where(square, jnp.broadcast_to(counts[...].astype(F32), (bricks, bricks)), 0.0),
        axis=1,
        keepdims=True,
    )
    for k in range(voxels // 512):
        voxel = (lax.broadcasted_iota(jnp.int32, (bricks, 512), 1) + k * 512).astype(F32)
        mask[:, k * 512 : (k + 1) * 512] = jnp.where(voxel < count_column, 1.0, 0.0).astype(BF16)

    def step_sums(t):
        for k in range(chunks):
            span = slice(k * CHUNK, (k + 1) * CHUNK)
            for copy in loads[t, k]:
                copy.wait()
            valid = mask[:, span]
            g = [image[t, c, :, span] * valid for c in range(COMPS)]
            r = resid[t, :, span]
            products = [g[c] * g[e] for c, e in PAIRS] + [g[c] * r for c in range(COMPS)]
            part = dot_nt(table[:, span], jnp.concatenate(products, axis=0))
            if k == 0:
                acc[...] = part
            else:
                acc[...] += part
        pairs = len(PAIRS) * bricks
        hess = acc[0:32, :pairs] + acc[32:64, :pairs]
        grad = acc[64:72, pairs:] + acc[72:80, pairs:]
        grad = jnp.concatenate([grad, jnp.zeros((8, bricks), F32)], axis=1)
        rows = []
        for q in range(len(PAIRS)):
            two = hess[:, 128 * (q // 2) : 128 * (q // 2) + 128]
            rows.append(pltpu.roll(two, 64, 1) if q % 2 else two)
        for c in range(COMPS):
            two = grad[:, 128 * (c // 2) : 128 * (c // 2) + 128]
            rows.append(pltpu.roll(two, 64, 1) if c % 2 else two)
        rows.append(jnp.zeros((LANES - GRAD_LANE - 24, 128), F32))
        return jnp.concatenate(rows, axis=0)

    sums = step_sums(1)

    for copy in small[1:3]:
        copy.wait()
    who = jnp.broadcast_to(owner[...].astype(F32), (8, bricks))
    earlier = lax.broadcasted_iota(jnp.int32, (bricks, bricks), 0) < lax.broadcasted_iota(
        jnp.int32, (bricks, bricks), 1
    )
    ones_before = jnp.dot(
        who.astype(BF16), jnp.where(earlier, 1.0, 0.0).astype(BF16), preferred_element_type=F32
    )
    place = lax.broadcasted_iota(jnp.int32, (8, bricks), 1).astype(F32)
    rank = jnp.where(who > 0.5, ones_before, place - ones_before)
    mine_first = jnp.where(s == 0, who, 1.0 - who)
    target = (mine_first * cap + rank)[0:1, :]
    slot = lax.broadcasted_iota(jnp.int32, (2 * cap, bricks), 0).astype(F32)
    hit = jnp.where(slot == jnp.broadcast_to(target, (2 * cap, bricks)), 1.0, 0.0)
    hit = jnp.concatenate([hit, jnp.zeros((2 * cap, 128 - bricks), F32)], axis=1).astype(BF16)

    def placed(x):
        a, b, c = split3(x)
        return dot_nt(hit, a) + dot_nt(hit, b) + dot_nt(hit, c)

    first = jnp.where(has_before, 0.0, 1.0)
    last = jnp.where(has_after, 0.0, 1.0)

    def weights(t):
        u = phase[t]
        v = 1.0 - u
        return (
            v * v * v * (1.0 / 6.0),
            (3.0 * u * u * u - 6.0 * u * u + 4.0) * (1.0 / 6.0),
            (-3.0 * u * u * u + 3.0 * u * u + 3.0 * u + 1.0) * (1.0 / 6.0),
            u * u * u * (1.0 / 6.0),
        )

    w = weights(0)
    basis0 = (w[0] * (1.0 - first), w[1] + first * w[0], w[2] + last * w[3], w[3] * (1.0 - last))
    w = weights(1)
    basis1 = (w[0], w[1] + last * (w[2] + w[3]), w[2] * (1.0 - last), w[3] * (1.0 - last))
    is_hess = lax.broadcasted_iota(jnp.int32, (1, LANES), 1) < GRAD_LANE

    def scale(b):
        return jnp.where(is_hess, b * b, b)

    def remote(src, dst, send_sem, recv_sem, where):
        return pltpu.make_async_remote_copy(
            src_ref=src,
            dst_ref=dst,
            send_sem=send_sem,
            recv_sem=recv_sem,
            device_id=where,
            device_id_type=MESH,
        )

    cores = (s, 1 - s)

    def to_after(k, i):
        return remote(
            send_fwd.at[k, i],
            recv_fwd.at[k, s],
            fwd_send_sem.at[k, i],
            fwd_recv_sem.at[k, s],
            (d + 1, cores[i]),
        )

    def to_before(i):
        return remote(
            send_back.at[i],
            recv_back.at[s],
            back_send_sem.at[i],
            back_recv_sem.at[s],
            (d - 1, cores[i]),
        )

    side = remote(send_side, mine.at[s], side_sem.at[0], side_sem.at[1], (d, 1 - s))

    placed1 = placed(sums)
    ahead = placed1 * scale(basis1[3])
    for i in range(2):
        send_fwd[1, i] = ahead[i * cap : (i + 1) * cap]

    pl.semaphore_wait(barrier, 1 + 2 * has_before.astype(jnp.int32) + 2 * has_after.astype(jnp.int32))

    @pl.when(jnp.logical_not(has_before))
    def _():
        recv_fwd[...] = jnp.zeros(recv_fwd.shape, F32)

    @pl.when(has_after)
    def _():
        for i in range(2):
            to_after(1, i).start()

    @pl.when(jnp.logical_not(has_after))
    def _():
        recv_back[...] = jnp.zeros(recv_back.shape, F32)

    sums = step_sums(0)
    placed0 = placed(sums)
    ahead = placed0 * scale(basis0[3]) + placed1 * scale(basis1[2])
    behind = placed0 * scale(basis0[0])
    for i in range(2):
        send_fwd[0, i] = ahead[i * cap : (i + 1) * cap]
        send_back[i] = behind[i * cap : (i + 1) * cap]

    @pl.when(has_after)
    def _():
        for i in range(2):
            to_after(0, i).start()

    @pl.when(has_before)
    def _():
        for i in range(2):
            to_before(i).start()

    for k in range(2):
        own = placed0 * scale(basis0[1 + k]) + placed1 * scale(basis1[k])
        mine[s, k] = own[:cap]
        send_side[k] = own[cap:]
    side.start()

    for copy in small[3:]:
        copy.wait()
    side.wait_send()
    remote(send_side, mine.at[1 - s], side_sem.at[0], side_sem.at[1], (d, 1 - s)).wait_recv()

    @pl.when(has_after)
    def _():
        for i in range(2):
            to_after(1, i).wait_send()
            to_after(0, i).wait_send()
            remote(
                send_back.at[i],
                recv_back.at[i],
                back_send_sem.at[i],
                back_recv_sem.at[i],
                (d + 1, i),
            ).wait_recv()

    @pl.when(has_before)
    def _():
        for i in range(2):
            to_before(i).wait_send()
            for k in range(2):
                remote(
                    send_fwd.at[k, i],
                    recv_fwd.at[k, i],
                    fwd_send_sem.at[k, i],
                    fwd_recv_sem.at[k, i],
                    (d - 1, i),
                ).wait_recv()

    for k in range(2):
        total = [mine[i, k] + recv_fwd[k, i] for i in range(2)]
        if k == 1:
            total = [total[i] + recv_back[i] for i in range(2)]
        parts = split3(jnp.concatenate(total, axis=0))
        table_h = spread[...]
        hess_ref[k] = sum(jnp.dot(part, table_h, preferred_element_type=F32) for part in parts)
        grad_ref[k] = sum(dot_nt(pick[...], part) for part in parts)


def per_device(n, n_space, image_gradient, residual, phase, counts, owner):
    steps, bricks, comps, voxels = image_gradient.shape
    cap = 3 * bricks // (2 * n_space)
    slots = n_space * cap
    hessian_lanes, gradient_lanes = spread_tables()
    hbm = pl.BlockSpec(memory_space=pltpu.HBM)
    vmem = pl.BlockSpec(memory_space=pltpu.VMEM)
    chunks = voxels // CHUNK
    dma = pltpu.SemaphoreType.DMA
    hess, grad = pl.pallas_call(
        functools.partial(kernel, n),
        out_shape=(
            jax.ShapeDtypeStruct((steps, slots, PATCH), F32),
            jax.ShapeDtypeStruct((steps, DOFS, slots), F32),
        ),
        in_specs=[hbm] * 8,
        out_specs=(vmem, vmem),
        scratch_shapes=[
            pltpu.VMEM((steps, comps, bricks, voxels), BF16),
            pltpu.VMEM((steps, bricks, voxels), BF16),
            pltpu.SMEM((steps,), F32),
            pltpu.VMEM((1, bricks), jnp.int32),
            pltpu.VMEM((1, bricks), jnp.int32),
            pltpu.VMEM((ROWS, voxels), BF16),
            pltpu.VMEM((LANES, PATCH), BF16),
            pltpu.VMEM((DOFS, LANES), BF16),
            pltpu.VMEM((bricks, voxels), BF16),
            pltpu.VMEM((ROWS, 9 * bricks), F32),
            pltpu.VMEM((2, 2, cap, LANES), F32),
            pltpu.VMEM((2, cap, LANES), F32),
            pltpu.VMEM((2, cap, LANES), F32),
            pltpu.VMEM((2, 2, cap, LANES), F32),
            pltpu.VMEM((2, cap, LANES), F32),
            pltpu.VMEM((2, 2, cap, LANES), F32),
            dma((3, 2, chunks)),
            dma((5,)),
            dma((2, 2)),
            dma((2, 2)),
            dma((2,)),
            dma((2,)),
            dma((2,)),
        ],
        compiler_params=pltpu.CompilerParams(
            collective_id=0, has_side_effects=True, vmem_limit_bytes=48 << 20
        ),
    )(
        jnp.transpose(image_gradient, (0, 2, 1, 3)),
        residual,
        phase,
        counts.reshape(1, bricks),
        owner.reshape(1, bricks),
        moment_table(),
        hessian_lanes,
        gradient_lanes,
    )
    return hess, jnp.transpose(grad, (0, 2, 1))


def solution(mesh):
    in_specs = (
        P("tm", "space", None, None),
        P("tm", "space", None),
        P("tm"),
        P("space"),
        P("space", None),
    )
    out_specs = (P("tm", "space", None), P("tm", "space", None))
    return jax.shard_map(
        functools.partial(per_device, mesh.shape["tm"], mesh.shape["space"]),
        mesh=mesh,
        in_specs=in_specs,
        out_specs=out_specs,
        check_vma=False,
    )
```

time: 134 us -> 26.2 us (0.20)
  the two profiles are of different devices: /device:TPU:255 before, /device:TPU:1 now
where the time goes in v1:
time: 26.2 us; the launch traced here: 25.9 us
  Pallas kernels  16 us (61%)
  local copies, waits for them, and re-layouts  9.22 us (35%)
  between operations  0.66 us (3%)
    pallas_call x1, Pallas kernels, per_device(): pl.pallas_call(functools.partial(kernel, n), out_shape=(jax.ShapeDtypeStr...  16 us
    unnamed x18, local copies, waits for them, and re-layouts  9.22 us

profile of v1, /device:TPU:1, one launch (start us, length us, event | category | flops | bytes accessed | tf_op | source)
XLA Modules:
  0.0 25.9 jit_solution(11757148996826006399)
XLA Ops:
  0.6 0.0 copy-start
  0.6 1.9 %copy-done = bf16[2,64,3,4096]{3,1,2,0:T(8,128)(2,1)S(1)} copy-done((bf16[2,64,3,4096]{3,1,2,0:T(8,128)(2,1)S(1)}, bf16[2,64,3,4096]{3,1,2,0:T(8,128)(2,1)}, u32[]{:S(2)}) %copy-start) | copy-done | bytes 3145752
  2.5 0.0 copy-start.1
  2.5 1.2 %copy-done.1 = bf16[2,64,4096]{2,1,0:T(8,128)(2,1)S(1)} copy-done((bf16[2,64,4096]{2,1,0:T(8,128)(2,1)S(1)}, bf16[2,64,4096]{2,1,0:T(8,128)(2,1)}, u32[]{:S(2)}) %copy-start.1) | copy-done | bytes 1048600
  3.7 0.0 copy-start.2
  3.7 1.1 %copy-done.2 = bf16[80,4096]{1,0:T(8,128)(2,1)S(1)} copy-done((bf16[80,4096]{1,0:T(8,128)(2,1)S(1)}, bf16[80,4096]{1,0:T(8,128)(2,1)}, u32[]{:S(2)}) %copy-start.2) | copy-done | bytes 655384
  4.8 0.0 copy-start.3
  4.8 1.0 %copy-done.3 = bf16[256,576]{1,0:T(8,128)(2,1)S(1)} copy-done((bf16[256,576]{1,0:T(8,128)(2,1)S(1)}, bf16[256,576]{1,0:T(8,128)(2,1)}, u32[]{:S(2)}) %copy-start.3) | copy-done | bytes 294936
  5.8 0.0 copy-start.4
  5.8 0.7 %copy-done.4 = bf16[24,256]{1,0:T(8,128)(2,1)S(1)} copy-done((bf16[24,256]{1,0:T(8,128)(2,1)S(1)}, bf16[24,256]{1,0:T(8,128)(2,1)}, u32[]{:S(2)}) %copy-start.4) | copy-done | bytes 12312
  6.5 0.0 copy-start.5
  6.5 0.7 %copy-done.5 = f32[2]{0:T(128)S(1)} copy-done((f32[2]{0:T(128)S(1)}, f32[2]{0:T(128)}, u32[]{:S(2)}) %copy-start.5) | copy-done | bytes 32
  7.2 0.0 copy-start.6
  7.2 0.7 %copy-done.6 = s32[64]{0:T(128)S(1)} copy-done((s32[64]{0:T(128)S(1)}, s32[64]{0:T(128)}, u32[]{:S(2)}) %copy-start.6) | copy-done | bytes 280
  7.8 0.0 copy-start.7
  7.8 0.7 %copy-done.7 = s32[64,1]{0,1:T(1,128)S(1)} copy-done((s32[64,1]{0,1:T(1,128)S(1)}, s32[64,1]{0,1:T(1,128)}, u32[]{:S(2)}) %copy-start.7) | copy-done | bytes 280
  8.5 16.0 %shard_map.95 = (f32[2,96,576]{2,1,0:T(8,128)S(1)}, f32[2,24,96]{2,1,0:T(8,128)S(1)}) custom-call(bf16[2,3,64,4096]{3,2,1,0:T(8,128)(2,1)S(1)} %bitcast.4, bf16[2,64,4096]{2,1,0:T(8,128)(2,1)S(1)} %copy-done.1, f32[2]{0:T(128)S(1)} %copy-done.5, s32[1,64]{1,0:T(1,128)S(1)} %bitcast.6, s32[1,64]{1,0:T(1,128)S(1)} %bitcast.7, bf16[80,4096]{1,0:T(8,128)(2,1)S(1)} %copy-done.2, ...), custom_call_target="tpu_custom_call" | custom-call | tf_op jit(solution)/shard_map/pallas_call | solution.py:376
  24.5 0.8 %copy.12 = f32[2,96,576]{2,1,0:T(8,128)} copy(f32[2,96,576]{2,1,0:T(8,128)S(1)} %get-tuple-element.8) | data formatting | bytes 884736
  25.3 0.6 %copy.13 = f32[2,96,24]{1,2,0:T(8,128)} copy(f32[2,96,24]{1,2,0:T(8,128)S(1)} %bitcast.5) | data formatting | bytes 36864
Async XLA Ops:
  0.6 1.9 %copy-start = (bf16[2,64,3,4096]{3,1,2,0:T(8,128)(2,1)S(1)}, bf16[2,64,3,4096]{3,1,2,0:T(8,128)(2,1)}, u32[]{:S(2)}) copy-start(bf16[2,64,3,4096]{3,1,2,0:T(8,128)(2,1)} %param.8) | copy-start | bytes 9437188
  2.5 1.2 %copy-start.1 = (bf16[2,64,4096]{2,1,0:T(8,128)(2,1)S(1)}, bf16[2,64,4096]{2,1,0:T(8,128)(2,1)}, u32[]{:S(2)}) copy-start(bf16[2,64,4096]{2,1,0:T(8,128)(2,1)} %resid_hbm.1) | copy-start | bytes 3145732
  3.7 1.1 %copy-start.2 = (bf16[80,4096]{1,0:T(8,128)(2,1)S(1)}, bf16[80,4096]{1,0:T(8,128)(2,1)}, u32[]{:S(2)}) copy-start(bf16[80,4096]{1,0:T(8,128)(2,1)} %constant.6.clone.table_hbm) | copy-start | bytes 1966084
  4.8 1.0 %copy-start.3 = (bf16[256,576]{1,0:T(8,128)(2,1)S(1)}, bf16[256,576]{1,0:T(8,128)(2,1)}, u32[]{:S(2)}) copy-start(bf16[256,576]{1,0:T(8,128)(2,1)} %constant.7.clone.spread_hbm) | copy-start | bytes 884740
  5.8 0.7 %copy-start.4 = (bf16[24,256]{1,0:T(8,128)(2,1)S(1)}, bf16[24,256]{1,0:T(8,128)(2,1)}, u32[]{:S(2)}) copy-start(bf16[24,256]{1,0:T(8,128)(2,1)} %constant.8.clone.pick_hbm) | copy-start | bytes 36868
  6.5 0.7 %copy-start.5 = (f32[2]{0:T(128)S(1)}, f32[2]{0:T(128)}, u32[]{:S(2)}) copy-start(f32[2]{0:T(128)} %phase_hbm.1) | copy-start | bytes 28
  7.2 0.7 %copy-start.6 = (s32[64]{0:T(128)S(1)}, s32[64]{0:T(128)}, u32[]{:S(2)}) copy-start(s32[64]{0:T(128)} %param.11) | copy-start | bytes 772
  7.8 0.7 %copy-start.7 = (s32[64,1]{0,1:T(1,128)S(1)}, s32[64,1]{0,1:T(1,128)}, u32[]{:S(2)}) copy-start(s32[64,1]{0,1:T(1,128)} %param.12) | copy-start | bytes 772

commit v2 on v1

--- a/solution.py
+++ b/solution.py
@@ -407,7 +407,7 @@
             dma((2,)),
         ],
         compiler_params=pltpu.CompilerParams(
-            collective_id=0, has_side_effects=True, vmem_limit_bytes=48 << 20
+            collective_id=0, has_side_effects=True, vmem_limit_bytes=67043328
         ),
     )(
         jnp.transpose(image_gradient, (0, 2, 1, 3)),

time: 26.2 us -> 21.8 us (0.83)
  the two profiles are of different devices: /device:TPU:1 before, /device:TPU:3 now
where the time goes in v2:
time: 21.8 us; the launch traced here: 21.6 us
  Pallas kernels  17.7 us (81%)
  local copies, waits for them, and re-layouts  3.19 us (15%)
  between operations  0.64 us (3%)
    pallas_call x1, Pallas kernels, per_device(): pl.pallas_call(functools.partial(kernel, n), out_shape=(jax.ShapeDtypeStr...  17.7 us
    unnamed x2, local copies, waits for them, and re-layouts  3.19 us

profile of v2, /device:TPU:3, one launch (start us, length us, event | category | flops | bytes accessed | tf_op | source)
XLA Modules:
  0.0 21.6 jit_solution(1333150578599857203)
XLA Ops:
  0.6 17.7 %shard_map.95 = (f32[2,96,576]{2,1,0:T(8,128)}, f32[2,24,96]{2,1,0:T(8,128)}) custom-call(bf16[2,3,64,4096]{3,2,1,0:T(8,128)(2,1)} %bitcast.4, bf16[2,64,4096]{2,1,0:T(8,128)(2,1)} %resid_hbm.1, f32[2]{0:T(128)} %phase_hbm.1, s32[1,64]{1,0:T(1,128)} %bitcast.6, s32[1,64]{1,0:T(1,128)} %bitcast.7, bf16[80,4096]{1,0:T(8,128)(2,1)} %constant.6.clone.table_hbm, ...), custom_call_target="tpu_custom_call" | custom-call | tf_op jit(solution)/shard_map/pallas_call | solution.py:376
  18.4 1.8 %copy.12 = f32[2,96,576]{2,1,0:T(8,128)} copy(f32[2,96,576]{2,1,0:T(8,128)} %get-tuple-element.8) | data formatting | bytes 884736
  20.2 1.3 %copy.13 = f32[2,96,24]{1,2,0:T(8,128)} copy(f32[2,96,24]{1,2,0:T(8,128)} %bitcast.5) | data formatting | bytes 36864

commit v3 on v2

--- a/solution.py
+++ b/solution.py
@@ -79,16 +79,15 @@
     table_hbm,
     spread_hbm,
     pick_hbm,
-    hess_ref,
-    grad_ref,
+    total_ref,
+    spread,
+    pick,
     image,
     resid,
     phase,
     counts,
     owner,
     table,
-    spread,
-    pick,
     mask,
     acc,
     send_fwd,
@@ -354,14 +353,33 @@
                     (d - 1, i),
                 ).wait_recv()
 
+    for i in range(2):
+        rows = slice(i * cap, (i + 1) * cap)
+        total_ref[0, rows] = mine[i, 0] + recv_fwd[0, i]
+        total_ref[1, rows] = mine[i, 1] + recv_fwd[1, i] + recv_back[i]
+
+
+def spread_kernel(total_ref, spread, pick, hess_hbm, grad_hbm, hess, grad, sem):
+    slots = total_ref.shape[1]
+    half = slots // 2
+    copies = []
+
+    def store(src, dst):
+        copies.append(pltpu.make_async_copy(src, dst, sem.at[len(copies)]))
+        copies[-1].start()
+
     for k in range(2):
-        total = [mine[i, k] + recv_fwd[k, i] for i in range(2)]
-        if k == 1:
-            total = [total[i] + recv_back[i] for i in range(2)]
-        parts = split3(jnp.concatenate(total, axis=0))
-        table_h = spread[...]
-        hess_ref[k] = sum(jnp.dot(part, table_h, preferred_element_type=F32) for part in parts)
-        grad_ref[k] = sum(dot_nt(pick[...], part) for part in parts)
+        parts = split3(total_ref[k])
+        for i in range(2):
+            rows = slice(i * half, (i + 1) * half)
+            hess[k, rows] = sum(
+                jnp.dot(part[rows], spread[...], preferred_element_type=F32) for part in parts
+            )
+            store(hess.at[k, rows], hess_hbm.at[k, rows])
+        grad[k] = sum(dot_nt(pick[...], part) for part in parts)
+        store(grad.at[k], grad_hbm.at[k])
+    for copy in copies:
+        copy.wait()
 
 
 def per_device(n, n_space, image_gradient, residual, phase, counts, owner):
@@ -373,14 +391,15 @@
     vmem = pl.BlockSpec(memory_space=pltpu.VMEM)
     chunks = voxels // CHUNK
     dma = pltpu.SemaphoreType.DMA
-    hess, grad = pl.pallas_call(
+    totals, spread, pick = pl.pallas_call(
         functools.partial(kernel, n),
         out_shape=(
-            jax.ShapeDtypeStruct((steps, slots, PATCH), F32),
-            jax.ShapeDtypeStruct((steps, DOFS, slots), F32),
+            jax.ShapeDtypeStruct((steps, slots, LANES), F32),
+            jax.ShapeDtypeStruct((LANES, PATCH), BF16),
+            jax.ShapeDtypeStruct((DOFS, LANES), BF16),
         ),
         in_specs=[hbm] * 8,
-        out_specs=(vmem, vmem),
+        out_specs=(vmem, vmem, vmem),
         scratch_shapes=[
             pltpu.VMEM((steps, comps, bricks, voxels), BF16),
             pltpu.VMEM((steps, bricks, voxels), BF16),
@@ -388,8 +407,6 @@
             pltpu.VMEM((1, bricks), jnp.int32),
             pltpu.VMEM((1, bricks), jnp.int32),
             pltpu.VMEM((ROWS, voxels), BF16),
-            pltpu.VMEM((LANES, PATCH), BF16),
-            pltpu.VMEM((DOFS, LANES), BF16),
             pltpu.VMEM((bricks, voxels), BF16),
             pltpu.VMEM((ROWS, 9 * bricks), F32),
             pltpu.VMEM((2, 2, cap, LANES), F32),
@@ -407,18 +424,38 @@
             dma((2,)),
         ],
         compiler_params=pltpu.CompilerParams(
-            collective_id=0, has_side_effects=True, vmem_limit_bytes=67043328
+            collective_id=0, has_side_effects=True, vmem_limit_bytes=40 << 20
         ),
     )(
-        jnp.transpose(image_gradient, (0, 2, 1, 3)),
-        residual,
-        phase,
-        counts.reshape(1, bricks),
-        owner.reshape(1, bricks),
-        moment_table(),
-        hessian_lanes,
-        gradient_lanes,
-    )
+        *[
+            pltpu.with_memory_space_constraint(x, pltpu.HBM)
+            for x in (
+                jnp.transpose(image_gradient, (0, 2, 1, 3)),
+                residual,
+                phase,
+                counts.reshape(1, bricks),
+                owner.reshape(1, bricks),
+                jnp.asarray(moment_table()),
+                jnp.asarray(hessian_lanes),
+                jnp.asarray(gradient_lanes),
+            )
+        ]
+    )
+    hess, grad = pl.pallas_call(
+        spread_kernel,
+        out_shape=(
+            jax.ShapeDtypeStruct((steps, slots, PATCH), F32),
+            jax.ShapeDtypeStruct((steps, DOFS, slots), F32),
+        ),
+        in_specs=[vmem] * 3,
+        out_specs=(hbm, hbm),
+        scratch_shapes=[
+            pltpu.VMEM((steps, slots, PATCH), F32),
+            pltpu.VMEM((steps, DOFS, slots), F32),
+            dma((3 * steps,)),
+        ],
+        compiler_params=pltpu.CompilerParams(vmem_limit_bytes=16 << 20),
+    )(totals, spread, pick)
     return hess, jnp.transpose(grad, (0, 2, 1))
 
 

time: 21.8 us -> 18.6 us (0.85)
  local copies, waits for them, and re-layouts: 3.19 us -> 0 us
    unnamed x2 -> x0, local copies, waits for them, and re-layouts: 3.19 us -> none
    pallas_call x0 -> x1, Pallas kernels: none -> 1.47 us  [per_device(): pl.pallas_call(spread_kernel, out_shape=(jax.ShapeDtypeStruct((steps, slo...]
    pallas_call x1, Pallas kernels: 17.7 us -> 16.4 us  [per_device(): pl.pallas_call(functools.partial(kernel, n), out_shape=(jax.ShapeDtypeStr...]
where the time goes in v3:
time: 18.6 us; the launch traced here: 18.5 us
  Pallas kernels  17.8 us (96%)
  between operations  0.64 us (3%)
    pallas_call x1, Pallas kernels, per_device(): pl.pallas_call(functools.partial(kernel, n), out_shape=(jax.ShapeDtypeStr...  16.4 us
    pallas_call x1, Pallas kernels, per_device(): pl.pallas_call(spread_kernel, out_shape=(jax.ShapeDtypeStruct((steps, slo...  1.47 us

profile of v3, /device:TPU:3, one launch (start us, length us, event | category | flops | bytes accessed | tf_op | source)
XLA Modules:
  0.0 18.5 jit_solution(7717016507365812736)
XLA Ops:
  0.6 16.4 %shard_map.95 = (f32[2,96,256]{2,1,0:T(8,128)S(1)}, bf16[256,576]{1,0:T(8,128)(2,1)S(1)}, bf16[24,256]{1,0:T(8,128)(2,1)S(1)}) custom-call(bf16[2,3,64,4096]{3,2,1,0:T(8,128)(2,1)} %bitcast.4, bf16[2,64,4096]{2,1,0:T(8,128)(2,1)} %resid_hbm.1, f32[2]{0:T(128)} %phase_hbm.1, s32[1,64]{1,0:T(1,128)} %bitcast.5, s32[1,64]{1,0:T(1,128)} %bitcast.6, ...), custom_call_target="tpu_custom_call" | custom-call | tf_op jit(solution)/shard_map/pallas_call | solution.py:394
  17.0 1.5 %shard_map.96 = (f32[2,96,576]{2,1,0:T(8,128)}, f32[2,24,96]{2,1,0:T(8,128)}) custom-call(f32[2,96,256]{2,1,0:T(8,128)S(1)} %get-tuple-element.7.total_ref, bf16[256,576]{1,0:T(8,128)(2,1)S(1)} %get-tuple-element.8.spread, bf16[24,256]{1,0:T(8,128)(2,1)S(1)} %get-tuple-element.9.pick), custom_call_target="tpu_custom_call" | custom-call | tf_op jit(solution)/shard_map/pallas_call | solution.py:444

commit v4 on v3

--- a/solution.py
+++ b/solution.py
@@ -15,9 +15,8 @@
 PATCH = DOFS * DOFS
 MOMENTS = 27
 PAIRS = ((0, 0), (0, 1), (0, 2), (1, 1), (1, 2), (2, 2))
-ROWS = 80
-LANES = 256
-GRAD_LANE = 32 * len(PAIRS)
+TILE = 256
+BLOCK = 32
 CHUNK = 1024
 MESH = pl.DeviceIdType.MESH
 F32 = jnp.float32
@@ -35,26 +34,32 @@
     u = [(axis + 0.5) / EDGE for axis in axes]
     quads = [((1 - x) ** 2, x * (1 - x), x * x) for x in u]
     lines = [(1 - x, x) for x in u]
-    moments = np.stack([quads[0][m // 9] * quads[1][m // 3 % 3] * quads[2][m % 3] for m in range(MOMENTS)])
-    shapes = np.stack([lines[0][a >> 2 & 1] * lines[1][a >> 1 & 1] * lines[2][a & 1] for a in range(NODES)])
-    table = np.zeros((ROWS, EDGE**3), BF16)
-    table[0:MOMENTS], table[32 : 32 + MOMENTS] = two_terms(moments)
-    table[64:72], table[72:80] = two_terms(shapes)
-    return table
+    exact = np.zeros((EDGE**3, 128))
+    for block in range(4):
+        for m in range(MOMENTS):
+            exact[:, BLOCK * block + m] = quads[0][m // 9] * quads[1][m // 3 % 3] * quads[2][m % 3]
+        for i in range(4):
+            a = 4 * (block % 2) + i
+            exact[:, BLOCK * block + MOMENTS + i] = (
+                lines[0][a >> 2 & 1] * lines[1][a >> 1 & 1] * lines[2][a & 1]
+            )
+    return np.concatenate(two_terms(exact), axis=1)
 
 
 def spread_tables():
-    hessian = np.zeros((LANES, PATCH), np.float32)
-    gradient = np.zeros((DOFS, LANES), np.float32)
+    hessian = np.zeros((256, PATCH), np.float32)
+    gradient = np.zeros((DOFS, 256), np.float32)
     for a in range(NODES):
         for c in range(COMPS):
-            gradient[COMPS * a + c, GRAD_LANE + NODES * c + a] = 1.0
+            gradient[COMPS * a + c, BLOCK * (2 * c + a // 4) + MOMENTS + a % 4] = 1.0
             for b in range(NODES):
                 for e in range(COMPS):
                     pair = PAIRS.index((min(c, e), max(c, e)))
                     bits = [(a >> s & 1) + (b >> s & 1) for s in (2, 1, 0)]
                     moment = bits[0] * 9 + bits[1] * 3 + bits[2]
-                    hessian[32 * pair + moment, (COMPS * a + c) * DOFS + COMPS * b + e] = 1.0
+                    hessian[BLOCK * pair + moment, (COMPS * a + c) * DOFS + COMPS * b + e] = 1.0
+    hessian[192:] = hessian[128:192]
+    gradient[:, 192:] = gradient[:, 128:192]
     return hessian.astype(BF16), gradient.astype(BF16)
 
 
@@ -89,7 +94,6 @@
     owner,
     table,
     mask,
-    acc,
     send_fwd,
     send_back,
     send_side,
@@ -105,7 +109,8 @@
     side_sem,
 ):
     bricks, voxels = resid.shape[1], resid.shape[2]
-    cap = mine.shape[2]
+    cap = 2 * mine.shape[2] // 3
+    half = cap // 2
     chunks = voxels // CHUNK
     d = lax.axis_index("tm")
     s = lax.axis_index("space")
@@ -135,7 +140,7 @@
             if t == 1:
                 loads[t, k].append(
                     pltpu.make_async_copy(
-                        table_hbm.at[:, span], table.at[:, span], load_sem.at[2, t, k]
+                        table_hbm.at[span], table.at[span], load_sem.at[2, t, k]
                     )
                 )
             for copy in loads[t, k]:
@@ -173,56 +178,75 @@
         voxel = (lax.broadcasted_iota(jnp.int32, (bricks, 512), 1) + k * 512).astype(F32)
         mask[:, k * 512 : (k + 1) * 512] = jnp.where(voxel < count_column, 1.0, 0.0).astype(BF16)
 
+    lane = lax.broadcasted_iota(jnp.int32, (1, 128), 1)
+    spare = lane % BLOCK >= MOMENTS
+
     def step_sums(t):
-        for k in range(chunks):
-            span = slice(k * CHUNK, (k + 1) * CHUNK)
-            for copy in loads[t, k]:
-                copy.wait()
-            valid = mask[:, span]
-            g = [image[t, c, :, span] * valid for c in range(COMPS)]
-            r = resid[t, :, span]
-            products = [g[c] * g[e] for c, e in PAIRS] + [g[c] * r for c in range(COMPS)]
-            part = dot_nt(table[:, span], jnp.concatenate(products, axis=0))
-            if k == 0:
-                acc[...] = part
-            else:
-                acc[...] += part
-        pairs = len(PAIRS) * bricks
-        hess = acc[0:32, :pairs] + acc[32:64, :pairs]
-        grad = acc[64:72, pairs:] + acc[72:80, pairs:]
-        grad = jnp.concatenate([grad, jnp.zeros((8, bricks), F32)], axis=1)
-        rows = []
-        for q in range(len(PAIRS)):
-            two = hess[:, 128 * (q // 2) : 128 * (q // 2) + 128]
-            rows.append(pltpu.roll(two, 64, 1) if q % 2 else two)
-        for c in range(COMPS):
-            two = grad[:, 128 * (c // 2) : 128 * (c // 2) + 128]
-            rows.append(pltpu.roll(two, 64, 1) if c % 2 else two)
-        rows.append(jnp.zeros((LANES - GRAD_LANE - 24, 128), F32))
-        return jnp.concatenate(rows, axis=0)
+        def sums(*accs):
+            for tile in range(voxels // TILE):
+                if tile * TILE % CHUNK == 0:
+                    for copy in loads[t, tile * TILE // CHUNK]:
+                        copy.wait()
+                unit, staging = tile % 2, tile // 2 % 2
+                span = slice(tile * TILE, (tile + 1) * TILE)
+                pltpu.matmul_push_rhs(table[span, :], staging, unit)
+                valid = mask[:, span]
+                g = [image[t, c, :, span] * valid for c in range(COMPS)]
+                r = resid[t, :, span]
+                products = [g[c] * g[e] for c, e in PAIRS] + [g[c] * r for c in range(COMPS)]
+                for q, product in enumerate(products):
+                    pltpu.matmul_acc_lhs(accs[9 * unit + q], product, staging if q == 0 else None)
+            found = []
+            for q in range(9):
+                both = pltpu.matmul_pop(accs[q]) + pltpu.matmul_pop(accs[9 + q])
+                found.append(both[:, :128] + both[:, 128:])
+            return found
+
+        found = pl.run_scoped(
+            sums, *[pltpu.ACC(unit)((bricks, 256), F32) for unit in range(2) for _ in range(9)]
+        )
+        first = jnp.where(lane < 2 * BLOCK, found[6], found[7])
+        for q in range(4):
+            first = jnp.where(jnp.logical_and(lane // BLOCK == q, jnp.logical_not(spare)), found[q], first)
+        second = jnp.where(spare, found[8], jnp.where(lane // BLOCK % 2 == 0, found[4], found[5]))
+        return jnp.concatenate([first, second], axis=1)
 
     sums = step_sums(1)
 
     for copy in small[1:3]:
         copy.wait()
-    who = jnp.broadcast_to(owner[...].astype(F32), (8, bricks))
+    who = owner[...].astype(F32)
+    who_column = jnp.sum(
+        jnp.where(square, jnp.broadcast_to(who, (bricks, bricks)), 0.0), axis=1, keepdims=True
+    )
     earlier = lax.broadcasted_iota(jnp.int32, (bricks, bricks), 0) < lax.broadcasted_iota(
         jnp.int32, (bricks, bricks), 1
     )
-    ones_before = jnp.dot(
-        who.astype(BF16), jnp.where(earlier, 1.0, 0.0).astype(BF16), preferred_element_type=F32
-    )
-    place = lax.broadcasted_iota(jnp.int32, (8, bricks), 1).astype(F32)
+    ones_before = jnp.sum(jnp.where(earlier, who_column, 0.0), axis=0, keepdims=True)
+    place = lax.broadcasted_iota(jnp.int32, (1, bricks), 1).astype(F32)
     rank = jnp.where(who > 0.5, ones_before, place - ones_before)
     mine_first = jnp.where(s == 0, who, 1.0 - who)
-    target = (mine_first * cap + rank)[0:1, :]
+    target = mine_first * cap + rank
     slot = lax.broadcasted_iota(jnp.int32, (2 * cap, bricks), 0).astype(F32)
     hit = jnp.where(slot == jnp.broadcast_to(target, (2 * cap, bricks)), 1.0, 0.0)
-    hit = jnp.concatenate([hit, jnp.zeros((2 * cap, 128 - bricks), F32)], axis=1).astype(BF16)
+    hit = hit.astype(BF16)
+    hits = jnp.concatenate([hit, hit, hit, jnp.zeros_like(hit)], axis=1)
 
     def placed(x):
-        a, b, c = split3(x)
-        return dot_nt(hit, a) + dot_nt(hit, b) + dot_nt(hit, c)
+        def product(acc):
+            pltpu.matmul_push_rhs(
+                jnp.concatenate([*split3(x), jnp.zeros(x.shape, BF16)], axis=0), 0, 0
+            )
+            pltpu.matmul_acc_lhs(acc, hits, 0)
+            return pltpu.matmul_pop(acc)
+
+        rows = pl.run_scoped(product, pltpu.ACC(0)((2 * cap, 256), F32))
+        out = []
+        for i in range(2):
+            part = rows[i * cap : (i + 1) * cap]
+            out.append(part[:, :128])
+            out.append(jnp.where(lane < 64, part[:half, 128:], part[half:, 128:]))
+        return jnp.concatenate(out, axis=0)
 
     first = jnp.where(has_before, 0.0, 1.0)
     last = jnp.where(has_after, 0.0, 1.0)
@@ -241,10 +265,10 @@
     basis0 = (w[0] * (1.0 - first), w[1] + first * w[0], w[2] + last * w[3], w[3] * (1.0 - last))
     w = weights(1)
     basis1 = (w[0], w[1] + last * (w[2] + w[3]), w[2] * (1.0 - last), w[3] * (1.0 - last))
-    is_hess = lax.broadcasted_iota(jnp.int32, (1, LANES), 1) < GRAD_LANE
+    size = cap + half
 
     def scale(b):
-        return jnp.where(is_hess, b * b, b)
+        return jnp.where(spare, b, b * b)
 
     def remote(src, dst, send_sem, recv_sem, where):
         return pltpu.make_async_remote_copy(
@@ -281,7 +305,7 @@
     placed1 = placed(sums)
     ahead = placed1 * scale(basis1[3])
     for i in range(2):
-        send_fwd[1, i] = ahead[i * cap : (i + 1) * cap]
+        send_fwd[1, i] = ahead[i * size : (i + 1) * size]
 
     pl.semaphore_wait(barrier, 1 + 2 * has_before.astype(jnp.int32) + 2 * has_after.astype(jnp.int32))
 
@@ -303,8 +327,8 @@
     ahead = placed0 * scale(basis0[3]) + placed1 * scale(basis1[2])
     behind = placed0 * scale(basis0[0])
     for i in range(2):
-        send_fwd[0, i] = ahead[i * cap : (i + 1) * cap]
-        send_back[i] = behind[i * cap : (i + 1) * cap]
+        send_fwd[0, i] = ahead[i * size : (i + 1) * size]
+        send_back[i] = behind[i * size : (i + 1) * size]
 
     @pl.when(has_after)
     def _():
@@ -318,20 +342,17 @@
 
     for k in range(2):
         own = placed0 * scale(basis0[1 + k]) + placed1 * scale(basis1[k])
-        mine[s, k] = own[:cap]
-        send_side[k] = own[cap:]
+        mine[s, k] = own[:size]
+        send_side[k] = own[size:]
     side.start()
 
     for copy in small[3:]:
         copy.wait()
-    side.wait_send()
     remote(send_side, mine.at[1 - s], side_sem.at[0], side_sem.at[1], (d, 1 - s)).wait_recv()
 
     @pl.when(has_after)
     def _():
         for i in range(2):
-            to_after(1, i).wait_send()
-            to_after(0, i).wait_send()
             remote(
                 send_back.at[i],
                 recv_back.at[i],
@@ -343,7 +364,6 @@
     @pl.when(has_before)
     def _():
         for i in range(2):
-            to_before(i).wait_send()
             for k in range(2):
                 remote(
                     send_fwd.at[k, i],
@@ -354,14 +374,27 @@
                 ).wait_recv()
 
     for i in range(2):
-        rows = slice(i * cap, (i + 1) * cap)
-        total_ref[0, rows] = mine[i, 0] + recv_fwd[0, i]
-        total_ref[1, rows] = mine[i, 1] + recv_fwd[1, i] + recv_back[i]
+        total_ref[0, i] = mine[i, 0] + recv_fwd[0, i]
+        total_ref[1, i] = mine[i, 1] + recv_fwd[1, i] + recv_back[i]
+
+    side.wait_send()
+
+    @pl.when(has_after)
+    def _():
+        for i in range(2):
+            to_after(1, i).wait_send()
+            to_after(0, i).wait_send()
+
+    @pl.when(has_before)
+    def _():
+        for i in range(2):
+            to_before(i).wait_send()
 
 
 def spread_kernel(total_ref, spread, pick, hess_hbm, grad_hbm, hess, grad, sem):
-    slots = total_ref.shape[1]
-    half = slots // 2
+    cap = 2 * total_ref.shape[2] // 3
+    half = cap // 2
+    lane = lax.broadcasted_iota(jnp.int32, (1, 128), 1)
     copies = []
 
     def store(src, dst):
@@ -369,9 +402,17 @@
         copies[-1].start()
 
     for k in range(2):
-        parts = split3(total_ref[k])
-        for i in range(2):
-            rows = slice(i * half, (i + 1) * half)
+        wide = []
+        for i in range(2):
+            tail = total_ref[k, i, cap:]
+            for j in range(2):
+                kept = jnp.where((lane < 64) == (j == 0), tail, 0.0)
+                wide.append(
+                    jnp.concatenate([total_ref[k, i, j * half : (j + 1) * half], kept], axis=1)
+                )
+        parts = split3(jnp.concatenate(wide, axis=0))
+        for i in range(2):
+            rows = slice(i * cap, (i + 1) * cap)
             hess[k, rows] = sum(
                 jnp.dot(part[rows], spread[...], preferred_element_type=F32) for part in parts
             )
@@ -386,6 +427,7 @@
     steps, bricks, comps, voxels = image_gradient.shape
     cap = 3 * bricks // (2 * n_space)
     slots = n_space * cap
+    size = cap + cap // 2
     hessian_lanes, gradient_lanes = spread_tables()
     hbm = pl.BlockSpec(memory_space=pltpu.HBM)
     vmem = pl.BlockSpec(memory_space=pltpu.VMEM)
@@ -394,9 +436,9 @@
     totals, spread, pick = pl.pallas_call(
         functools.partial(kernel, n),
         out_shape=(
-            jax.ShapeDtypeStruct((steps, slots, LANES), F32),
-            jax.ShapeDtypeStruct((LANES, PATCH), BF16),
-            jax.ShapeDtypeStruct((DOFS, LANES), BF16),
+            jax.ShapeDtypeStruct((steps, 2, size, 128), F32),
+            jax.ShapeDtypeStruct((256, PATCH), BF16),
+            jax.ShapeDtypeStruct((DOFS, 256), BF16),
         ),
         in_specs=[hbm] * 8,
         out_specs=(vmem, vmem, vmem),
@@ -406,15 +448,14 @@
             pltpu.SMEM((steps,), F32),
             pltpu.VMEM((1, bricks), jnp.int32),
             pltpu.VMEM((1, bricks), jnp.int32),
-            pltpu.VMEM((ROWS, voxels), BF16),
+            pltpu.VMEM((voxels, 256), BF16),
             pltpu.VMEM((bricks, voxels), BF16),
-            pltpu.VMEM((ROWS, 9 * bricks), F32),
-            pltpu.VMEM((2, 2, cap, LANES), F32),
-            pltpu.VMEM((2, cap, LANES), F32),
-            pltpu.VMEM((2, cap, LANES), F32),
-            pltpu.VMEM((2, 2, cap, LANES), F32),
-            pltpu.VMEM((2, cap, LANES), F32),
-            pltpu.VMEM((2, 2, cap, LANES), F32),
+            pltpu.VMEM((2, 2, size, 128), F32),
+            pltpu.VMEM((2, size, 128), F32),
+            pltpu.VMEM((2, size, 128), F32),
+            pltpu.VMEM((2, 2, size, 128), F32),
+            pltpu.VMEM((2, size, 128), F32),
+            pltpu.VMEM((2, 2, size, 128), F32),
             dma((3, 2, chunks)),
             dma((5,)),
             dma((2, 2)),

time: 18.6 us -> 17.5 us (0.941)
  Pallas kernels: 17.8 us -> 16.8 us
    pallas_call x1, Pallas kernels: 16.4 us -> 15.3 us  [per_device(): pl.pallas_call(functools.partial(kernel, n), out_shape=(jax.ShapeDtypeStr...]
where the time goes in v4:
time: 17.5 us; the launch traced here: 17.4 us
  Pallas kernels  16.8 us (96%)
  between operations  0.64 us (4%)
    pallas_call x1, Pallas kernels, per_device(): pl.pallas_call(functools.partial(kernel, n), out_shape=(jax.ShapeDtypeStr...  15.3 us
    pallas_call x1, Pallas kernels, per_device(): pl.pallas_call(spread_kernel, out_shape=(jax.ShapeDtypeStruct((steps, slo...  1.47 us

profile of v4, /device:TPU:3, one launch (start us, length us, event | category | flops | bytes accessed | tf_op | source)
XLA Modules:
  0.0 17.4 jit_solution(3860018102570080659)
XLA Ops:
  0.6 15.3 %shard_map.95 = (f32[2,2,72,128]{3,2,1,0:T(8,128)S(1)}, bf16[256,576]{1,0:T(8,128)(2,1)S(1)}, bf16[24,256]{1,0:T(8,128)(2,1)S(1)}) custom-call(bf16[2,3,64,4096]{3,2,1,0:T(8,128)(2,1)} %bitcast.4, bf16[2,64,4096]{2,1,0:T(8,128)(2,1)} %resid_hbm.1, f32[2]{0:T(128)} %phase_hbm.1, s32[1,64]{1,0:T(1,128)} %bitcast.5, s32[1,64]{1,0:T(1,128)} %bitcast.6, ...), custom_call_target="tpu_custom_call" | custom-call | tf_op jit(solution)/shard_map/pallas_call | solution.py:436
  16.0 1.5 %shard_map.96 = (f32[2,96,576]{2,1,0:T(8,128)}, f32[2,24,96]{2,1,0:T(8,128)}) custom-call(f32[2,2,72,128]{3,2,1,0:T(8,128)S(1)} %get-tuple-element.7.total_ref, bf16[256,576]{1,0:T(8,128)(2,1)S(1)} %get-tuple-element.8.spread, bf16[24,256]{1,0:T(8,128)(2,1)S(1)} %get-tuple-element.9.pick), custom_call_target="tpu_custom_call" | custom-call | tf_op jit(solution)/shard_map/pallas_call | solution.py:485

commit v5 on v4

--- a/solution.py
+++ b/solution.py
@@ -17,7 +17,8 @@
 PAIRS = ((0, 0), (0, 1), (0, 2), (1, 1), (1, 2), (2, 2))
 TILE = 256
 BLOCK = 32
-CHUNK = 1024
+CHUNKS = ((2048, 2048), (1024, 1024, 2048))
+AHEAD = 6
 MESH = pl.DeviceIdType.MESH
 F32 = jnp.float32
 BF16 = jnp.bfloat16
@@ -68,6 +69,11 @@
     rest = x - first.astype(F32)
     second = rest.astype(BF16)
     return first, second, (rest - second.astype(F32)).astype(BF16)
+
+
+def split2(x):
+    first = x.astype(BF16)
+    return first, (x - first.astype(F32)).astype(BF16)
 
 
 def dot_nt(a, b):
@@ -111,7 +117,6 @@
     bricks, voxels = resid.shape[1], resid.shape[2]
     cap = 2 * mine.shape[2] // 3
     half = cap // 2
-    chunks = voxels // CHUNK
     d = lax.axis_index("tm")
     s = lax.axis_index("space")
     has_before = d > 0
@@ -127,8 +132,8 @@
     small[0].start()
     loads = {}
     for t in (1, 0):
-        for k in range(chunks):
-            span = pl.ds(k * CHUNK, CHUNK)
+        for k, size in enumerate(CHUNKS[t]):
+            span = pl.ds(sum(CHUNKS[t][:k]), size)
             loads[t, k] = [
                 pltpu.make_async_copy(
                     image_hbm.at[t, :, :, span], image.at[t, :, :, span], load_sem.at[0, t, k]
@@ -181,37 +186,32 @@
     lane = lax.broadcasted_iota(jnp.int32, (1, 128), 1)
     spare = lane % BLOCK >= MOMENTS
 
-    def step_sums(t):
-        def sums(*accs):
-            for tile in range(voxels // TILE):
-                if tile * TILE % CHUNK == 0:
-                    for copy in loads[t, tile * TILE // CHUNK]:
-                        copy.wait()
-                unit, staging = tile % 2, tile // 2 % 2
-                span = slice(tile * TILE, (tile + 1) * TILE)
-                pltpu.matmul_push_rhs(table[span, :], staging, unit)
-                valid = mask[:, span]
-                g = [image[t, c, :, span] * valid for c in range(COMPS)]
-                r = resid[t, :, span]
-                products = [g[c] * g[e] for c, e in PAIRS] + [g[c] * r for c in range(COMPS)]
-                for q, product in enumerate(products):
-                    pltpu.matmul_acc_lhs(accs[9 * unit + q], product, staging if q == 0 else None)
-            found = []
-            for q in range(9):
-                both = pltpu.matmul_pop(accs[q]) + pltpu.matmul_pop(accs[9 + q])
-                found.append(both[:, :128] + both[:, 128:])
-            return found
-
-        found = pl.run_scoped(
-            sums, *[pltpu.ACC(unit)((bricks, 256), F32) for unit in range(2) for _ in range(9)]
-        )
+    def add_tiles(t, accs, begin, end):
+        for tile in range(begin, end):
+            unit, staging = tile % 2, tile // 2 % 2
+            span = slice(tile * TILE, (tile + 1) * TILE)
+            pltpu.matmul_push_rhs(table[span, :], staging, unit)
+            valid = mask[:, span]
+            g = [image[t, c, :, span] * valid for c in range(COMPS)]
+            r = resid[t, :, span]
+            products = [g[c] * g[e] for c, e in PAIRS] + [g[c] * r for c in range(COMPS)]
+            for q, product in enumerate(products):
+                pltpu.matmul_acc_lhs(accs[9 * unit + q], product, staging if q == 0 else None)
+
+    def pop_sums(accs):
+        found = []
+        for q in range(9):
+            both = pltpu.matmul_pop(accs[q]) + pltpu.matmul_pop(accs[9 + q])
+            found.append(both[:, :128] + both[:, 128:])
+        return found
+
+    def arranged(found):
         first = jnp.where(lane < 2 * BLOCK, found[6], found[7])
         for q in range(4):
             first = jnp.where(jnp.logical_and(lane // BLOCK == q, jnp.logical_not(spare)), found[q], first)
         second = jnp.where(spare, found[8], jnp.where(lane // BLOCK % 2 == 0, found[4], found[5]))
         return jnp.concatenate([first, second], axis=1)
 
-    sums = step_sums(1)
 
     for copy in small[1:3]:
         copy.wait()
@@ -232,15 +232,12 @@
     hit = hit.astype(BF16)
     hits = jnp.concatenate([hit, hit, hit, jnp.zeros_like(hit)], axis=1)
 
-    def placed(x):
-        def product(acc):
-            pltpu.matmul_push_rhs(
-                jnp.concatenate([*split3(x), jnp.zeros(x.shape, BF16)], axis=0), 0, 0
-            )
-            pltpu.matmul_acc_lhs(acc, hits, 0)
-            return pltpu.matmul_pop(acc)
-
-        rows = pl.run_scoped(product, pltpu.ACC(0)((2 * cap, 256), F32))
+    def placed(x, acc):
+        pltpu.matmul_push_rhs(
+            jnp.concatenate([*split3(x), jnp.zeros(x.shape, BF16)], axis=0), 0, 0
+        )
+        pltpu.matmul_acc_lhs(acc, hits, 0)
+        rows = pltpu.matmul_pop(acc)
         out = []
         for i in range(2):
             part = rows[i * cap : (i + 1) * cap]
@@ -302,28 +299,50 @@
 
     side = remote(send_side, mine.at[s], side_sem.at[0], side_sem.at[1], (d, 1 - s))
 
-    placed1 = placed(sums)
-    ahead = placed1 * scale(basis1[3])
-    for i in range(2):
-        send_fwd[1, i] = ahead[i * size : (i + 1) * size]
-
-    pl.semaphore_wait(barrier, 1 + 2 * has_before.astype(jnp.int32) + 2 * has_after.astype(jnp.int32))
-
-    @pl.when(jnp.logical_not(has_before))
-    def _():
-        recv_fwd[...] = jnp.zeros(recv_fwd.shape, F32)
-
-    @pl.when(has_after)
-    def _():
-        for i in range(2):
-            to_after(1, i).start()
-
-    @pl.when(jnp.logical_not(has_after))
-    def _():
-        recv_back[...] = jnp.zeros(recv_back.shape, F32)
-
-    sums = step_sums(0)
-    placed0 = placed(sums)
+    def send_second(placed1):
+        ahead = placed1 * scale(basis1[3])
+        for i in range(2):
+            send_fwd[1, i] = ahead[i * size : (i + 1) * size]
+
+        pl.semaphore_wait(barrier, 1 + 2 * has_before.astype(jnp.int32) + 2 * has_after.astype(jnp.int32))
+
+        @pl.when(jnp.logical_not(has_before))
+        def _():
+            recv_fwd[...] = jnp.zeros(recv_fwd.shape, F32)
+
+        @pl.when(has_after)
+        def _():
+            for i in range(2):
+                to_after(1, i).start()
+
+        @pl.when(jnp.logical_not(has_after))
+        def _():
+            recv_back[...] = jnp.zeros(recv_back.shape, F32)
+
+    tiles = voxels // TILE
+
+    def second_step(*accs):
+        done = 0
+        for k, voxel_count in enumerate(CHUNKS[1]):
+            for copy in loads[1, k]:
+                copy.wait()
+            add_tiles(1, accs, done, done + voxel_count // TILE)
+            done += voxel_count // TILE
+        return pop_sums(accs)
+
+    def first_step(place_acc, *accs):
+        for k in range(len(CHUNKS[0])):
+            for copy in loads[0, k]:
+                copy.wait()
+        add_tiles(0, accs, 0, AHEAD)
+        placed1 = placed(arranged(found), place_acc)
+        send_second(placed1)
+        add_tiles(0, accs, AHEAD, tiles)
+        return placed1, placed(arranged(pop_sums(accs)), place_acc)
+
+    sums_acc = [pltpu.ACC(unit)((bricks, 256), F32) for unit in range(2) for _ in range(9)]
+    found = pl.run_scoped(second_step, *sums_acc)
+    placed1, placed0 = pl.run_scoped(first_step, pltpu.ACC(0)((2 * cap, 256), F32), *sums_acc)
     ahead = placed0 * scale(basis0[3]) + placed1 * scale(basis1[2])
     behind = placed0 * scale(basis0[0])
     for i in range(2):
@@ -410,14 +429,12 @@
                 wide.append(
                     jnp.concatenate([total_ref[k, i, j * half : (j + 1) * half], kept], axis=1)
                 )
-        parts = split3(jnp.concatenate(wide, axis=0))
-        for i in range(2):
-            rows = slice(i * cap, (i + 1) * cap)
-            hess[k, rows] = sum(
-                jnp.dot(part[rows], spread[...], preferred_element_type=F32) for part in parts
-            )
-            store(hess.at[k, rows], hess_hbm.at[k, rows])
-        grad[k] = sum(dot_nt(pick[...], part) for part in parts)
+        both = jnp.concatenate(split2(jnp.concatenate(wide, axis=0)), axis=0)
+        slots = 2 * cap
+        spread_both = jnp.dot(both, spread[...], preferred_element_type=F32)
+        hess[k] = spread_both[:slots] + spread_both[slots:]
+        store(hess.at[k], hess_hbm.at[k])
+        grad[k] = dot_nt(pick[...], both[:slots]) + dot_nt(pick[...], both[slots:])
         store(grad.at[k], grad_hbm.at[k])
     for copy in copies:
         copy.wait()
@@ -431,7 +448,7 @@
     hessian_lanes, gradient_lanes = spread_tables()
     hbm = pl.BlockSpec(memory_space=pltpu.HBM)
     vmem = pl.BlockSpec(memory_space=pltpu.VMEM)
-    chunks = voxels // CHUNK
+    chunks = max(map(len, CHUNKS))
     dma = pltpu.SemaphoreType.DMA
     totals, spread, pick = pl.pallas_call(
         functools.partial(kernel, n),
@@ -493,7 +510,7 @@
         scratch_shapes=[
             pltpu.VMEM((steps, slots, PATCH), F32),
             pltpu.VMEM((steps, DOFS, slots), F32),
-            dma((3 * steps,)),
+            dma((2 * steps,)),
         ],
         compiler_params=pltpu.CompilerParams(vmem_limit_bytes=16 << 20),
     )(totals, spread, pick)

time: 17.5 us -> 17 us (0.971)
  the two profiles are of different devices: /device:TPU:3 before, /device:TPU:385 now
where the time goes in v5:
time: 17 us; the launch traced here: 16.9 us
  Pallas kernels  16.2 us (95%)
  between operations  0.64 us (4%)
    pallas_call x1, Pallas kernels, per_device(): pl.pallas_call(functools.partial(kernel, n), out_shape=(jax.ShapeDtypeStr...  15.1 us
    pallas_call x1, Pallas kernels, per_device(): pl.pallas_call(spread_kernel, out_shape=(jax.ShapeDtypeStruct((steps, slo...  1.11 us

profile of v5, /device:TPU:385, one launch (start us, length us, event | category | flops | bytes accessed | tf_op | source)
XLA Modules:
  0.0 16.9 jit_solution(580241501605687700)
XLA Ops:
  0.6 15.1 %shard_map.95 = (f32[2,2,72,128]{3,2,1,0:T(8,128)S(1)}, bf16[256,576]{1,0:T(8,128)(2,1)S(1)}, bf16[24,256]{1,0:T(8,128)(2,1)S(1)}) custom-call(bf16[2,3,64,4096]{3,2,1,0:T(8,128)(2,1)} %bitcast.4, bf16[2,64,4096]{2,1,0:T(8,128)(2,1)} %resid_hbm.1, f32[2]{0:T(128)} %phase_hbm.1, s32[1,64]{1,0:T(1,128)} %bitcast.5, s32[1,64]{1,0:T(1,128)} %bitcast.6, ...), custom_call_target="tpu_custom_call" | custom-call | tf_op jit(solution)/shard_map/pallas_call | solution.py:453
  15.8 1.1 %shard_map.96 = (f32[2,96,576]{2,1,0:T(8,128)}, f32[2,24,96]{2,1,0:T(8,128)}) custom-call(f32[2,2,72,128]{3,2,1,0:T(8,128)S(1)} %get-tuple-element.7.total_ref, bf16[256,576]{1,0:T(8,128)(2,1)S(1)} %get-tuple-element.8.spread, bf16[24,256]{1,0:T(8,128)(2,1)S(1)} %get-tuple-element.9.pick), custom_call_target="tpu_custom_call" | custom-call | tf_op jit(solution)/shard_map/pallas_call | solution.py:502

commit v6 on v5

--- a/solution.py
+++ b/solution.py
@@ -17,7 +17,8 @@
 PAIRS = ((0, 0), (0, 1), (0, 2), (1, 1), (1, 2), (2, 2))
 TILE = 256
 BLOCK = 32
-CHUNKS = ((2048, 2048), (1024, 1024, 2048))
+CHUNKS = ((2048, 2048), (2048, 2048))
+EARLY = 2
 AHEAD = 6
 MESH = pl.DeviceIdType.MESH
 F32 = jnp.float32
@@ -35,12 +36,12 @@
     u = [(axis + 0.5) / EDGE for axis in axes]
     quads = [((1 - x) ** 2, x * (1 - x), x * x) for x in u]
     lines = [(1 - x, x) for x in u]
-    exact = np.zeros((EDGE**3, 128))
-    for block in range(4):
+    exact = np.zeros((EDGE**3, 2 * BLOCK))
+    for block in range(2):
         for m in range(MOMENTS):
             exact[:, BLOCK * block + m] = quads[0][m // 9] * quads[1][m // 3 % 3] * quads[2][m % 3]
         for i in range(4):
-            a = 4 * (block % 2) + i
+            a = 4 * block + i
             exact[:, BLOCK * block + MOMENTS + i] = (
                 lines[0][a >> 2 & 1] * lines[1][a >> 1 & 1] * lines[2][a & 1]
             )
@@ -148,10 +149,12 @@
                         table_hbm.at[span], table.at[span], load_sem.at[2, t, k]
                     )
                 )
-            for copy in loads[t, k]:
-                copy.start()
-    for copy in small[1:]:
-        copy.start()
+            if t == 1 and k < EARLY:
+                for copy in loads[t, k]:
+                    copy.start()
+            if t == 1 and k == 0:
+                for copy in small[1:3]:
+                    copy.start()
 
     barrier = pltpu.get_barrier_semaphore()
 
@@ -170,19 +173,19 @@
         greet((d + 1, 0))
         greet((d + 1, 1))
 
-    small[0].wait()
+    for copy in small[:3]:
+        copy.wait()
     square = lax.broadcasted_iota(jnp.int32, (bricks, bricks), 0) == lax.broadcasted_iota(
         jnp.int32, (bricks, bricks), 1
     )
-    count_column = jnp.sum(
-        jnp.where(square, jnp.broadcast_to(counts[...].astype(F32), (bricks, bricks)), 0.0),
-        axis=1,
-        keepdims=True,
-    )
-    for k in range(voxels // 512):
-        voxel = (lax.broadcasted_iota(jnp.int32, (bricks, 512), 1) + k * 512).astype(F32)
-        mask[:, k * 512 : (k + 1) * 512] = jnp.where(voxel < count_column, 1.0, 0.0).astype(BF16)
-
+
+    def column(row):
+        return jnp.sum(
+            jnp.where(square, jnp.broadcast_to(row, (bricks, bricks)), 0.0), axis=1, keepdims=True
+        )
+
+    count = jnp.broadcast_to(column(counts[...].astype(F32)), (bricks, TILE))
+    voxel = lax.broadcasted_iota(jnp.int32, (bricks, TILE), 1).astype(F32)
     lane = lax.broadcasted_iota(jnp.int32, (1, 128), 1)
     spare = lane % BLOCK >= MOMENTS
 
@@ -190,7 +193,10 @@
         for tile in range(begin, end):
             unit, staging = tile % 2, tile // 2 % 2
             span = slice(tile * TILE, (tile + 1) * TILE)
-            pltpu.matmul_push_rhs(table[span, :], staging, unit)
+            part = table[span, :]
+            pltpu.matmul_push_rhs(jnp.concatenate([part, part], axis=1), staging, unit)
+            if t == 1:
+                mask[:, span] = jnp.where(voxel < count - tile * TILE, 1.0, 0.0).astype(BF16)
             valid = mask[:, span]
             g = [image[t, c, :, span] * valid for c in range(COMPS)]
             r = resid[t, :, span]
@@ -201,8 +207,8 @@
     def pop_sums(accs):
         found = []
         for q in range(9):
-            both = pltpu.matmul_pop(accs[q]) + pltpu.matmul_pop(accs[9 + q])
-            found.append(both[:, :128] + both[:, 128:])
+            both = (pltpu.matmul_pop(accs[q]) + pltpu.matmul_pop(accs[9 + q]))[:, :128]
+            found.append(both + pltpu.roll(both, 64, 1))
         return found
 
     def arranged(found):
@@ -213,26 +219,23 @@
         return jnp.concatenate([first, second], axis=1)
 
 
-    for copy in small[1:3]:
-        copy.wait()
-    who = owner[...].astype(F32)
-    who_column = jnp.sum(
-        jnp.where(square, jnp.broadcast_to(who, (bricks, bricks)), 0.0), axis=1, keepdims=True
-    )
-    earlier = lax.broadcasted_iota(jnp.int32, (bricks, bricks), 0) < lax.broadcasted_iota(
-        jnp.int32, (bricks, bricks), 1
-    )
-    ones_before = jnp.sum(jnp.where(earlier, who_column, 0.0), axis=0, keepdims=True)
-    place = lax.broadcasted_iota(jnp.int32, (1, bricks), 1).astype(F32)
-    rank = jnp.where(who > 0.5, ones_before, place - ones_before)
-    mine_first = jnp.where(s == 0, who, 1.0 - who)
-    target = mine_first * cap + rank
-    slot = lax.broadcasted_iota(jnp.int32, (2 * cap, bricks), 0).astype(F32)
-    hit = jnp.where(slot == jnp.broadcast_to(target, (2 * cap, bricks)), 1.0, 0.0)
-    hit = hit.astype(BF16)
-    hits = jnp.concatenate([hit, hit, hit, jnp.zeros_like(hit)], axis=1)
-
-    def placed(x, acc):
+    def slot_table():
+        who = owner[...].astype(F32)
+        who_column = column(who)
+        earlier = lax.broadcasted_iota(jnp.int32, (bricks, bricks), 0) < lax.broadcasted_iota(
+            jnp.int32, (bricks, bricks), 1
+        )
+        ones_before = jnp.sum(jnp.where(earlier, who_column, 0.0), axis=0, keepdims=True)
+        place = lax.broadcasted_iota(jnp.int32, (1, bricks), 1).astype(F32)
+        rank = jnp.where(who > 0.5, ones_before, place - ones_before)
+        mine_first = jnp.where(s == 0, who, 1.0 - who)
+        target = mine_first * cap + rank
+        slot = lax.broadcasted_iota(jnp.int32, (2 * cap, bricks), 0).astype(F32)
+        hit = jnp.where(slot == jnp.broadcast_to(target, (2 * cap, bricks)), 1.0, 0.0)
+        hit = hit.astype(BF16)
+        return jnp.concatenate([hit, hit, hit, jnp.zeros_like(hit)], axis=1)
+
+    def placed(x, hits, acc):
         pltpu.matmul_push_rhs(
             jnp.concatenate([*split3(x), jnp.zeros(x.shape, BF16)], axis=0), 0, 0
         )
@@ -326,33 +329,43 @@
         for k, voxel_count in enumerate(CHUNKS[1]):
             for copy in loads[1, k]:
                 copy.wait()
+            if k == 0:
+                for later in [(1, j) for j in range(EARLY, len(CHUNKS[1]))] + [(0, j) for j in range(len(CHUNKS[0]))]:
+                    for copy in loads[later]:
+                        copy.start()
+                for copy in small[3:]:
+                    copy.start()
             add_tiles(1, accs, done, done + voxel_count // TILE)
             done += voxel_count // TILE
-        return pop_sums(accs)
+            if k == 0:
+                hits = slot_table()
+        return hits, pop_sums(accs)
 
     def first_step(place_acc, *accs):
         for k in range(len(CHUNKS[0])):
             for copy in loads[0, k]:
                 copy.wait()
         add_tiles(0, accs, 0, AHEAD)
-        placed1 = placed(arranged(found), place_acc)
+        placed1 = placed(arranged(found), hits, place_acc)
         send_second(placed1)
         add_tiles(0, accs, AHEAD, tiles)
-        return placed1, placed(arranged(pop_sums(accs)), place_acc)
+        return placed1, placed(arranged(pop_sums(accs)), hits, place_acc)
 
     sums_acc = [pltpu.ACC(unit)((bricks, 256), F32) for unit in range(2) for _ in range(9)]
-    found = pl.run_scoped(second_step, *sums_acc)
+    hits, found = pl.run_scoped(second_step, *sums_acc)
     placed1, placed0 = pl.run_scoped(first_step, pltpu.ACC(0)((2 * cap, 256), F32), *sums_acc)
     ahead = placed0 * scale(basis0[3]) + placed1 * scale(basis1[2])
+    for i in range(2):
+        send_fwd[0, i] = ahead[i * size : (i + 1) * size]
+
+    @pl.when(has_after)
+    def _():
+        for i in range(2):
+            to_after(0, i).start()
+
     behind = placed0 * scale(basis0[0])
     for i in range(2):
-        send_fwd[0, i] = ahead[i * size : (i + 1) * size]
         send_back[i] = behind[i * size : (i + 1) * size]
-
-    @pl.when(has_after)
-    def _():
-        for i in range(2):
-            to_after(0, i).start()
 
     @pl.when(has_before)
     def _():
@@ -465,7 +478,7 @@
             pltpu.SMEM((steps,), F32),
             pltpu.VMEM((1, bricks), jnp.int32),
             pltpu.VMEM((1, bricks), jnp.int32),
-            pltpu.VMEM((voxels, 256), BF16),
+            pltpu.VMEM((voxels, 128), BF16),
             pltpu.VMEM((bricks, voxels), BF16),
             pltpu.VMEM((2, 2, size, 128), F32),
             pltpu.VMEM((2, size, 128), F32),

time: 17 us -> 16.2 us (0.953)
  Pallas kernels: 16.2 us -> 15.4 us
    pallas_call x1, Pallas kernels: 15.1 us -> 14.3 us  [per_device(): pl.pallas_call(functools.partial(kernel, n), out_shape=(jax.ShapeDtypeStr...]
where the time goes in v6:
time: 16.2 us; the launch traced here: 16 us
  Pallas kernels  15.4 us (95%)
  between operations  0.64 us (4%)
    pallas_call x1, Pallas kernels, per_device(): pl.pallas_call(functools.partial(kernel, n), out_shape=(jax.ShapeDtypeStr...  14.3 us
    pallas_call x1, Pallas kernels, per_device(): pl.pallas_call(spread_kernel, out_shape=(jax.ShapeDtypeStruct((steps, slo...  1.1 us

profile of v6, /device:TPU:385, one launch (start us, length us, event | category | flops | bytes accessed | tf_op | source)
XLA Modules:
  0.0 16.0 jit_solution(708506131883822453)
XLA Ops:
  0.6 14.3 %shard_map.95 = (f32[2,2,72,128]{3,2,1,0:T(8,128)S(1)}, bf16[256,576]{1,0:T(8,128)(2,1)S(1)}, bf16[24,256]{1,0:T(8,128)(2,1)S(1)}) custom-call(bf16[2,3,64,4096]{3,2,1,0:T(8,128)(2,1)} %bitcast.4, bf16[2,64,4096]{2,1,0:T(8,128)(2,1)} %resid_hbm.1, f32[2]{0:T(128)} %phase_hbm.1, s32[1,64]{1,0:T(1,128)} %bitcast.5, s32[1,64]{1,0:T(1,128)} %bitcast.6, ...), custom_call_target="tpu_custom_call" | custom-call | tf_op jit(solution)/shard_map/pallas_call | solution.py:466
  14.9 1.1 %shard_map.96 = (f32[2,96,576]{2,1,0:T(8,128)}, f32[2,24,96]{2,1,0:T(8,128)}) custom-call(f32[2,2,72,128]{3,2,1,0:T(8,128)S(1)} %get-tuple-element.7.total_ref, bf16[256,576]{1,0:T(8,128)(2,1)S(1)} %get-tuple-element.8.spread, bf16[24,256]{1,0:T(8,128)(2,1)S(1)} %get-tuple-element.9.pick), custom_call_target="tpu_custom_call" | custom-call | tf_op jit(solution)/shard_map/pallas_call | solution.py:515

commit v7 on v6

--- a/solution.py
+++ b/solution.py
@@ -17,7 +17,7 @@
 PAIRS = ((0, 0), (0, 1), (0, 2), (1, 1), (1, 2), (2, 2))
 TILE = 256
 BLOCK = 32
-CHUNKS = ((2048, 2048), (2048, 2048))
+CHUNKS = ((2048, 2048), (1024, 3072))
 EARLY = 2
 AHEAD = 6
 MESH = pl.DeviceIdType.MESH
@@ -205,17 +205,18 @@
                 pltpu.matmul_acc_lhs(accs[9 * unit + q], product, staging if q == 0 else None)
 
     def pop_sums(accs):
-        found = []
-        for q in range(9):
-            both = (pltpu.matmul_pop(accs[q]) + pltpu.matmul_pop(accs[9 + q]))[:, :128]
-            found.append(both + pltpu.roll(both, 64, 1))
-        return found
+        return [
+            (pltpu.matmul_pop(accs[q]) + pltpu.matmul_pop(accs[9 + q]))[:, :128] for q in range(9)
+        ]
 
     def arranged(found):
-        first = jnp.where(lane < 2 * BLOCK, found[6], found[7])
-        for q in range(4):
-            first = jnp.where(jnp.logical_and(lane // BLOCK == q, jnp.logical_not(spare)), found[q], first)
-        second = jnp.where(spare, found[8], jnp.where(lane // BLOCK % 2 == 0, found[4], found[5]))
+        twos = []
+        for c in range(COMPS):
+            two = jnp.where(lane // BLOCK % 2 == 0, found[2 * c], found[2 * c + 1])
+            two = jnp.where(spare, found[6 + c], two)
+            twos.append(two + pltpu.roll(two, 64, 1))
+        first = jnp.where(lane < 64, twos[0], twos[1])
+        second = twos[2]
         return jnp.concatenate([first, second], axis=1)
 
 
@@ -235,11 +236,13 @@
         hit = hit.astype(BF16)
         return jnp.concatenate([hit, hit, hit, jnp.zeros_like(hit)], axis=1)
 
-    def placed(x, hits, acc):
+    def start_place(x, hits, acc):
         pltpu.matmul_push_rhs(
             jnp.concatenate([*split3(x), jnp.zeros(x.shape, BF16)], axis=0), 0, 0
         )
         pltpu.matmul_acc_lhs(acc, hits, 0)
+
+    def placed(acc):
         rows = pltpu.matmul_pop(acc)
         out = []
         for i in range(2):
@@ -346,10 +349,13 @@
             for copy in loads[0, k]:
                 copy.wait()
         add_tiles(0, accs, 0, AHEAD)
-        placed1 = placed(arranged(found), hits, place_acc)
+        start_place(arranged(found), hits, place_acc)
+        add_tiles(0, accs, AHEAD, 2 * AHEAD)
+        placed1 = placed(place_acc)
         send_second(placed1)
-        add_tiles(0, accs, AHEAD, tiles)
-        return placed1, placed(arranged(pop_sums(accs)), hits, place_acc)
+        add_tiles(0, accs, 2 * AHEAD, tiles)
+        start_place(arranged(pop_sums(accs)), hits, place_acc)
+        return placed1, placed(place_acc)
 
     sums_acc = [pltpu.ACC(unit)((bricks, 256), F32) for unit in range(2) for _ in range(9)]
     hits, found = pl.run_scoped(second_step, *sums_acc)

time: 16.2 us -> 16.4 us (1.012)
  the two profiles are of different devices: /device:TPU:385 before, /device:TPU:321 now
where the time goes in v7:
time: 16.4 us; the launch traced here: 16.2 us
  Pallas kernels  15.6 us (95%)
  between operations  0.64 us (4%)
    pallas_call x1, Pallas kernels, per_device(): pl.pallas_call(functools.partial(kernel, n), out_shape=(jax.ShapeDtypeStr...  14.5 us
    pallas_call x1, Pallas kernels, per_device(): pl.pallas_call(spread_kernel, out_shape=(jax.ShapeDtypeStruct((steps, slo...  1.11 us

profile of v7, /device:TPU:321, one launch (start us, length us, event | category | flops | bytes accessed | tf_op | source)
XLA Modules:
  0.0 16.2 jit_solution(15766921345024790979)
XLA Ops:
  0.6 14.5 %shard_map.95 = (f32[2,2,72,128]{3,2,1,0:T(8,128)S(1)}, bf16[256,576]{1,0:T(8,128)(2,1)S(1)}, bf16[24,256]{1,0:T(8,128)(2,1)S(1)}) custom-call(bf16[2,3,64,4096]{3,2,1,0:T(8,128)(2,1)} %bitcast.4, bf16[2,64,4096]{2,1,0:T(8,128)(2,1)} %resid_hbm.1, f32[2]{0:T(128)} %phase_hbm.1, s32[1,64]{1,0:T(1,128)} %bitcast.5, s32[1,64]{1,0:T(1,128)} %bitcast.6, ...), custom_call_target="tpu_custom_call" | custom-call | tf_op jit(solution)/shard_map/pallas_call | solution.py:472
  15.1 1.1 %shard_map.96 = (f32[2,96,576]{2,1,0:T(8,128)}, f32[2,24,96]{2,1,0:T(8,128)}) custom-call(f32[2,2,72,128]{3,2,1,0:T(8,128)S(1)} %get-tuple-element.7.total_ref, bf16[256,576]{1,0:T(8,128)(2,1)S(1)} %get-tuple-element.8.spread, bf16[24,256]{1,0:T(8,128)(2,1)S(1)} %get-tuple-element.9.pick), custom_call_target="tpu_custom_call" | custom-call | tf_op jit(solution)/shard_map/pallas_call | solution.py:521

commit v8 on v7

--- a/solution.py
+++ b/solution.py
@@ -17,9 +17,9 @@
 PAIRS = ((0, 0), (0, 1), (0, 2), (1, 1), (1, 2), (2, 2))
 TILE = 256
 BLOCK = 32
-CHUNKS = ((2048, 2048), (1024, 3072))
+CHUNKS = ((2048, 2048), (2048, 2048))
 EARLY = 2
-AHEAD = 6
+AHEAD = 2
 MESH = pl.DeviceIdType.MESH
 F32 = jnp.float32
 BF16 = jnp.bfloat16

time: 16.4 us -> 15.9 us (0.970)
  the two profiles are of different devices: /device:TPU:321 before, /device:TPU:385 now
where the time goes in v8:
time: 15.9 us; the launch traced here: 15.8 us
  Pallas kernels  15.1 us (95%)
  between operations  0.64 us (4%)
    pallas_call x1, Pallas kernels, per_device(): pl.pallas_call(functools.partial(kernel, n), out_shape=(jax.ShapeDtypeStr...  14 us
    pallas_call x1, Pallas kernels, per_device(): pl.pallas_call(spread_kernel, out_shape=(jax.ShapeDtypeStruct((steps, slo...  1.11 us

profile of v8, /device:TPU:385, one launch (start us, length us, event | category | flops | bytes accessed | tf_op | source)
XLA Modules:
  0.0 15.8 jit_solution(12273593967332247593)
XLA Ops:
  0.6 14.0 %shard_map.95 = (f32[2,2,72,128]{3,2,1,0:T(8,128)S(1)}, bf16[256,576]{1,0:T(8,128)(2,1)S(1)}, bf16[24,256]{1,0:T(8,128)(2,1)S(1)}) custom-call(bf16[2,3,64,4096]{3,2,1,0:T(8,128)(2,1)} %bitcast.4, bf16[2,64,4096]{2,1,0:T(8,128)(2,1)} %resid_hbm.1, f32[2]{0:T(128)} %phase_hbm.1, s32[1,64]{1,0:T(1,128)} %bitcast.5, s32[1,64]{1,0:T(1,128)} %bitcast.6, ...), custom_call_target="tpu_custom_call" | custom-call | tf_op jit(solution)/shard_map/pallas_call | solution.py:472
  14.6 1.1 %shard_map.96 = (f32[2,96,576]{2,1,0:T(8,128)}, f32[2,24,96]{2,1,0:T(8,128)}) custom-call(f32[2,2,72,128]{3,2,1,0:T(8,128)S(1)} %get-tuple-element.7.total_ref, bf16[256,576]{1,0:T(8,128)(2,1)S(1)} %get-tuple-element.8.spread, bf16[24,256]{1,0:T(8,128)(2,1)S(1)} %get-tuple-element.9.pick), custom_call_target="tpu_custom_call" | custom-call | tf_op jit(solution)/shard_map/pallas_call | solution.py:521
